TPU v7x, 32 devices: a whole 2x2x4 slice. The times are simulated.
32 devices in a mesh: dp: 4 (over x, core), ctx: 8 (over z, y).
Axes of the slice: x: 2, y: 2, z: 4, core: 2. Of those that a mesh axis runs over, the one named last changes fastest.
Arguments:
- queries: bfloat16 [4, 2048, 1024], P('dp', 'ctx'), may hold values from -4.5 to 4.5
- keys: bfloat16 [4, 2048, 1024], P('dp', 'ctx'), may hold values from -4.5 to 4.5
- values: bfloat16 [4, 2048, 1024], P('dp', 'ctx'), may hold values from -6 to 6
- out_grad: bfloat16 [4, 2048, 2048], P('dp', 'ctx'), may hold values from -6 to 6
- chosen: int32 [4, 8], P('dp'), may hold values from -1 to 15, as said below
- proj: bfloat16 [1024, 2048], P('ctx', 'dp'), may hold values from -0.1875 to 0.1875
Outputs:
- attn_out: bfloat16 [4, 2048, 2048], P('dp', 'ctx')
- q_grad: bfloat16 [4, 2048, 1024], P('dp', 'ctx')
- k_grad: bfloat16 [4, 2048, 1024], P('dp', 'ctx')
- v_grad: bfloat16 [4, 2048, 1024], P('dp', 'ctx')
- proj_grad: float32 [1024, 2048], P('ctx', 'dp')
Inputs may be any that keep to these rules, and one draw needn't show every extreme that they name: chosen[d, c] is -1 or the index pos // 128 of one of the blocks that ctx index c stores (position spans c and 15 - c, of 1 block each); every sequence has one or more entries that are not -1.
All inputs are finite; a program needn't handle non-finite values.
Results may differ from a plain program's by a relative error of at most 0.023.
Values may be sent and summed in bfloat16 or wider, within the bound.
A program may use at most 192 MiB of HBM per device.

v0:
```python
import functools
import math

import jax
import jax.numpy as jnp
from jax import lax
from jax.experimental import pallas as pl
from jax.experimental.pallas import tpu as pltpu
from jax.sharding import PartitionSpec as P

BLOCK = 128
FAR = 1 << 30


def dot_nt(a, b):
    return lax.dot_general(a, b, (((1,), (1,)), ((), ())), preferred_element_type=jnp.float32)


def dot_nn(a, b):
    return lax.dot_general(a, b, (((1,), (0,)), ((), ())), preferred_element_type=jnp.float32)


def transposed(a):
    return a.astype(jnp.float32).T.astype(a.dtype)


def block_marks(picked, me, count):
    entry = picked[0, me]
    spans = count // 2
    index = jnp.maximum(entry, 0)
    local = jnp.where(index // spans == me, index % spans, spans + index % spans)
    local = jnp.where(entry >= 0, local, -1)
    return [jnp.where(local == j, 1.0, 0.0) for j in range(count)]


def place_kernel(n, dn, count, picked, mix, dq, dkv, w, out, q_out, k_out, v_out, w_out):
    marks = block_marks(picked, lax.axis_index("ctx"), count)
    block, dh, dc = dq.shape[1], dq.shape[2], mix.shape[2]
    for j, mark in enumerate(marks):
        rows = slice(j * block, (j + 1) * block)
        for h in range(n):
            cols = slice(h * dh, (h + 1) * dh)
            q_out[rows, cols] = (dq[h].astype(jnp.float32) * mark).astype(q_out.dtype)
            k_out[rows, cols] = (dkv[h, 0].astype(jnp.float32) * mark).astype(k_out.dtype)
            v_out[rows, cols] = (dkv[h, 1].astype(jnp.float32) * mark).astype(v_out.dtype)
        for d in range(dn):
            cols = slice(d * dc, (d + 1) * dc)
            out[rows, cols] = (mix[d].astype(jnp.float32) * mark).astype(out.dtype)
    w_out[...] = w[...]


def kernel(
    n, dn, scale,
    picked, q_in, k_in, v_in, g_in, proj,
    dq_r, dkv_r, w_out, mix_r,
    qkv, g, kpos, qkv_r, g_r, proj_r, agp_s, agp_r, ag_s, ag_r, attn_s, attn_r, attn_d, attn_t,
    p_s, k_t, v_t, dq_s, dkv_s, dk_acc, dv_acc, w_s, w_y, w_r, mix_s,
    qkv_ss, qkv_rs, g_ss, g_rs, proj_ss, proj_rs, fwd_ss, agp_ss, agp_rs, ag_ss, ag_rs,
    attn_ss, attn_rs, ad_ss, ad_rs, ad_fs, dq_ss, dq_rs, dkv_ss, dkv_rs, w_ss, wy_rs, w_rs, mix_ss, mix_rs,
    loc,
):
    me = lax.axis_index("ctx")
    md = lax.axis_index("dp")
    bf16 = jnp.bfloat16
    block, dh = qkv.shape[2], qkv.shape[3]
    dc = proj.shape[1]
    slots = n * block
    width = 2 * block
    steps = n // 2

    def ctx_copy(src, dst, ss, rs, peer):
        return pltpu.make_async_remote_copy(
            src_ref=src, dst_ref=dst, send_sem=ss, recv_sem=rs,
            device_id={"ctx": peer}, device_id_type=pl.DeviceIdType.MESH)

    def dp_copy(src, dst, ss, rs, peer):
        return pltpu.make_async_remote_copy(
            src_ref=src, dst_ref=dst, send_sem=ss, recv_sem=rs,
            device_id={"dp": peer}, device_id_type=pl.DeviceIdType.MESH)

    ctx_peers = [lax.rem(me + s, n) for s in range(1, n)]
    dp_peers = [lax.rem(md + s, dn) for s in range(1, dn)]

    barrier = pltpu.get_barrier_semaphore()
    for peer in ctx_peers:
        pl.semaphore_signal(barrier, inc=1, device_id={"ctx": peer}, device_id_type=pl.DeviceIdType.MESH)
    for peer in dp_peers:
        pl.semaphore_signal(barrier, inc=1, device_id={"dp": peer}, device_id_type=pl.DeviceIdType.MESH)

    own_proj = pltpu.make_async_copy(proj, proj_r.at[me], loc.at[2])
    own_proj.start()
    marks = block_marks(picked, me, q_in.shape[0] // block)

    def chosen_rows(ref, low, high):
        total = None
        for j, mark in enumerate(marks):
            term = ref[j * block:(j + 1) * block, low:high].astype(jnp.float32) * mark
            total = term if total is None else total + term
        return total.astype(bf16)

    pair = me + 1 - 2 * lax.rem(me, 2)
    far = [lax.rem(me + 2 * s, n) for s in range(1, n // 2)]
    pl.semaphore_wait(barrier, n - 1 + dn - 1)
    sends = []

    def go(copy):
        copy.start()
        sends.append(copy)

    for peer in far + [pair]:
        go(ctx_copy(proj, proj_r.at[me], proj_ss.at[peer], proj_rs.at[me], peer))
    for j in range(dn):
        g[j] = chosen_rows(g_in, j * dc, (j + 1) * dc)
    for peer in dp_peers:
        go(dp_copy(g.at[peer], g_r.at[md], g_ss.at[peer], g_rs.at[md], peer))
    g_r[md] = g[md]
    for t, ref in enumerate((q_in, k_in, v_in)):
        for h in range(n):
            qkv[h, t] = chosen_rows(ref, h * dh, (h + 1) * dh)
    qkv_r[me] = qkv[me]

    def send_qkv(peers):
        for peer in peers:
            go(ctx_copy(qkv.at[peer], qkv_r.at[me], qkv_ss.at[peer], qkv_rs.at[me], peer))

    pair_far = [lax.rem(pair + 2 * s, n) for s in range(1, n // 2)]
    down = lax.broadcasted_iota(jnp.int32, (block, block), 0)
    for j in range(n):
        entry = picked[0, j]
        kpos[j * block:(j + 1) * block] = down + jnp.where(entry >= 0, entry * block, FAR)
    own_proj.wait()

    def ctx_arrived(buf, ss, rs, peer):
        ctx_copy(buf.at[peer], buf.at[peer], ss.at[peer], rs.at[peer], peer).wait_recv()

    def dp_arrived(buf, ss, rs, peer):
        dp_copy(buf.at[peer], buf.at[peer], ss.at[peer], rs.at[peer], peer).wait_recv()

    for peer in dp_peers:
        dp_arrived(g_r, g_ss, g_rs, peer)

    def part(h):
        out = dot_nt(g_r[...].reshape(dn * block, dc), proj_r[h]).astype(bf16)
        agp_s[h] = out.reshape(dn, block, dh)
        for peer in dp_peers:
            go(dp_copy(agp_s.at[h, peer], agp_r.at[h, md], agp_ss.at[h, peer], agp_rs.at[h, md], peer))

    def finish(h):
        total = agp_s[h, md].astype(jnp.float32)
        for peer in dp_peers:
            dp_copy(agp_r.at[h, peer], agp_r.at[h, peer], agp_ss.at[h, peer], agp_rs.at[h, peer], peer).wait_recv()
            total = total + agp_r[h, peer].astype(jnp.float32)
        ag_s[h] = total.astype(bf16)
        if h is me:
            ag_r[me] = ag_s[me]
        else:
            go(ctx_copy(ag_s.at[h], ag_r.at[me], ag_ss.at[h], ag_rs.at[me], h))

    heads = [me, pair] + far + pair_far
    lag = 2
    for k, h in enumerate(heads):
        if k:
            ctx_arrived(proj_r, proj_ss, proj_rs, h)
        if 2 <= k < 2 + len(far):
            go(ctx_copy(proj_r.at[h], proj_r.at[h], fwd_ss.at[h], proj_rs.at[h], pair))
        part(h)
        if k == 1 + len(far):
            send_qkv(ctx_peers)
        if k >= lag:
            finish(heads[k - lag])
    for h in heads[-lag:]:
        finish(h)

    for peer in ctx_peers:
        ctx_arrived(qkv_r, qkv_ss, qkv_rs, peer)
    k_t[...] = transposed(qkv_r[:, 1].reshape(slots, dh))
    v_t[...] = transposed(qkv_r[:, 2].reshape(slots, dh))

    def send_pair(i, src, dst, ss, rs, own_sem):
        for half in range(2):
            peer = 2 * i + half

            @pl.when(peer != me)
            def _():
                ctx_copy(src.at[peer], dst.at[me], ss.at[peer], rs.at[me], peer).start()

            @pl.when(peer == me)
            def _():
                pltpu.make_async_copy(src.at[peer], dst.at[peer], own_sem).start()

    def forward(i, carry):
        q = qkv_r[pl.ds(2 * i, 2), 0].reshape(width, dh)
        k = qkv_r[:, 1].reshape(slots, dh)
        scores = dot_nt(k, q) * scale
        key_pos = kpos[...]
        key_pos = jnp.concatenate([key_pos, key_pos], axis=1)
        same = lax.broadcasted_iota(jnp.int32, (slots, width), 0) == (
            lax.broadcasted_iota(jnp.int32, (slots, width), 1) + i * width)
        lane = lax.broadcasted_iota(jnp.int32, (1, width), 1)
        first, second = picked[0, 2 * i], picked[0, 2 * i + 1]
        first = jnp.where(first >= 0, first * block, -FAR)
        second = jnp.where(second >= 0, (second - 1) * block, -FAR)
        query_pos = lane + jnp.where(lane < block, first, second)
        scores = jnp.where((key_pos <= query_pos) | same, scores, -1e30)
        e = jnp.exp(scores - jnp.max(scores, axis=0, keepdims=True))
        p = (e * (1.0 / jnp.sum(e, axis=0, keepdims=True))).astype(bf16)
        p_s[i] = p
        a_t = dot_nn(v_t[...], p)
        attn_t[i] = a_t.astype(bf16)
        attn_s[pl.ds(2 * i, 2)] = a_t.T.astype(bf16).reshape(2, block, dh)
        send_pair(i, attn_s, attn_r, attn_ss, attn_rs, loc.at[3])
        return carry

    lax.fori_loop(0, steps, forward, 0)

    for peer in ctx_peers:
        ctx_arrived(ag_r, ag_ss, ag_rs, peer)
    dk_acc[...] = jnp.zeros_like(dk_acc)
    dv_acc[...] = jnp.zeros_like(dv_acc)

    def backward(i, carry):
        q = qkv_r[pl.ds(2 * i, 2), 0].reshape(width, dh)
        v = qkv_r[:, 2].reshape(slots, dh)
        da = ag_r[pl.ds(2 * i, 2)].reshape(width, dh)
        delta = jnp.sum(da.astype(jnp.float32).T * attn_t[i].astype(jnp.float32), axis=0, keepdims=True)
        p = p_s[i]
        ds = (p.astype(jnp.float32) * (dot_nt(v, da) - delta)).astype(bf16)
        dq_t = dot_nn(k_t[...], ds) * scale
        dq_s[pl.ds(2 * i, 2)] = dq_t.T.astype(bf16).reshape(2, block, dh)
        send_pair(i, dq_s, dq_r, dq_ss, dq_rs, loc.at[4])
        dk_acc[...] += dot_nn(ds, q)
        dv_acc[...] += dot_nn(p, da)
        return carry

    early = steps // 2
    lax.fori_loop(0, early, backward, 0)
    for peer in ctx_peers:
        ctx_arrived(attn_r, attn_ss, attn_rs, peer)
    pltpu.make_async_copy(attn_s.at[me], attn_r.at[me], loc.at[3]).wait()
    twin = md + 1 - 2 * lax.rem(md, 2)
    dp_far = [lax.rem(md + 2 * s, dn) for s in range(1, dn // 2)]
    for peer in dp_far + [twin]:
        go(dp_copy(attn_r, attn_d.at[md], ad_ss.at[peer], ad_rs.at[md], peer))
    own_attn = pltpu.make_async_copy(attn_r, attn_d.at[md], loc.at[5])
    own_attn.start()
    lax.fori_loop(early, steps, backward, 0)

    dkv_s[:, 0] = (dk_acc[...] * scale).astype(bf16).reshape(n, block, dh)
    dkv_s[:, 1] = dv_acc[...].astype(bf16).reshape(n, block, dh)
    for peer in ctx_peers:
        go(ctx_copy(dkv_s.at[peer], dkv_r.at[me], dkv_ss.at[peer], dkv_rs.at[me], peer))
    dkv_r[me] = dkv_s[me]

    own_attn.wait()
    for peer in dp_far:
        dp_arrived(attn_d, ad_ss, ad_rs, peer)
        go(dp_copy(attn_d.at[peer], attn_d.at[peer], ad_fs.at[peer], ad_rs.at[peer], twin))
    for peer in [twin] + [lax.rem(twin + 2 * s, dn) for s in range(1, dn // 2)]:
        dp_arrived(attn_d, ad_ss, ad_rs, peer)

    def weight(h):
        heads = attn_d[:, h].reshape(dn * block, dh)
        return dot_nn(transposed(heads), g_r[...].reshape(dn * block, dc))

    side = lax.rem(me, 2)
    row = me // 2
    orders = [lax.rem(row + s, n // 2) for s in range(1, n // 2)] + [row]
    for a in orders:
        h = 2 * a + 1 - side
        w_s[h] = weight(h).astype(bf16)
        go(ctx_copy(w_s.at[h], w_y.at[a], w_ss.at[h], wy_rs.at[a], pair))

    def mix_step(j, carry):
        rows = jnp.concatenate(
            [attn_d[pl.ds(2 * j, 2), h].reshape(width, dh) for h in range(n)], axis=1)
        out = dot_nn(rows, proj_r[...].reshape(n * dh, dc))
        mix_s[pl.ds(2 * j, 2)] = out.astype(bf16).reshape(2, block, dc)
        return carry

    lax.fori_loop(0, dn // 2, mix_step, 0)
    for peer in dp_peers:
        go(dp_copy(mix_s.at[peer], mix_r.at[md], mix_ss.at[peer], mix_rs.at[md], peer))
    mix_r[md] = mix_s[md]

    for a in orders:
        h = 2 * a + side
        total = weight(h)
        ctx_copy(w_y.at[a], w_y.at[a], w_ss.at[h], wy_rs.at[a], pair).wait_recv()
        total = total + w_y[a].astype(jnp.float32)
        if a is row:
            w_out[...] = total
        else:
            w_s[h] = total.astype(bf16)
            go(ctx_copy(w_s.at[h], w_r.at[row], w_ss.at[h], w_rs.at[row], h))

    pltpu.make_async_copy(dq_s.at[me], dq_r.at[me], loc.at[4]).wait()
    for peer in ctx_peers:
        ctx_arrived(dq_r, dq_ss, dq_rs, peer)
    for peer in ctx_peers:
        ctx_arrived(dkv_r, dkv_ss, dkv_rs, peer)
    for a in orders[:-1]:
        ctx_copy(w_r.at[a], w_r.at[a], w_ss.at[a], w_rs.at[a], pair).wait_recv()
        w_out[...] += w_r[a].astype(jnp.float32)
    for peer in dp_peers:
        dp_arrived(mix_r, mix_ss, mix_rs, peer)

    for copy in sends:
        copy.wait_send()
    for peer in ctx_peers:
        ctx_copy(attn_s.at[peer], attn_r.at[me], attn_ss.at[peer], attn_rs.at[me], peer).wait_send()
        ctx_copy(dq_s.at[peer], dq_r.at[me], dq_ss.at[peer], dq_rs.at[me], peer).wait_send()


def shards(queries, keys, values, out_grad, chosen, proj):
    n = lax.axis_size("ctx")
    dn = lax.axis_size("dp")
    tokens = queries.shape[1]
    dh = queries.shape[2] // n
    dc = proj.shape[1]
    slots = n * BLOCK
    width = 2 * BLOCK
    steps = n // 2
    bf16, f32 = jnp.bfloat16, jnp.float32
    sem = pltpu.SemaphoreType.DMA
    vm = pltpu.VMEM
    blocks = (n, BLOCK, dh)
    scratch = [
        vm((n, 3, BLOCK, dh), bf16), vm((dn, BLOCK, dc), bf16), vm((slots, BLOCK), jnp.int32),
        vm((n, 3, BLOCK, dh), bf16), vm((dn, BLOCK, dc), bf16), vm((n, dh, dc), bf16),
        vm((n, dn, BLOCK, dh), bf16), vm((n, dn, BLOCK, dh), bf16), vm(blocks, bf16), vm(blocks, bf16),
        vm(blocks, bf16), vm(blocks, bf16), vm((dn,) + blocks, bf16), vm((steps, dh, width), bf16),
        vm((steps, slots, width), bf16), vm((dh, slots), bf16), vm((dh, slots), bf16),
        vm(blocks, bf16), vm((n, 2, BLOCK, dh), bf16), vm((slots, dh), f32), vm((slots, dh), f32),
        vm((n, dh, dc), bf16), vm((n // 2, dh, dc), bf16), vm((n // 2, dh, dc), bf16), vm((dn, BLOCK, dc), bf16),
    ]
    c, d = sem((n,)), sem((dn,))
    e = sem((n, dn))
    sems = [c, c, d, d, c, c, c, e, e, c, c, c, c, d, d, d, c, c, c, c, c, c, c, d, d, sem((6,))]
    vmem = pl.BlockSpec(memory_space=pltpu.VMEM)
    smem = pl.BlockSpec(memory_space=pltpu.SMEM)
    dq, dkv, weight_grad, mixed = pl.pallas_call(
        functools.partial(kernel, n, dn, 1.0 / math.sqrt(dh)),
        out_shape=(
            jax.ShapeDtypeStruct(blocks, bf16),
            jax.ShapeDtypeStruct((n, 2, BLOCK, dh), bf16),
            jax.ShapeDtypeStruct((dh, dc), f32),
            jax.ShapeDtypeStruct((dn, BLOCK, dc), bf16),
        ),
        in_specs=[smem] + [vmem] * 5,
        out_specs=[pl.BlockSpec(memory_space=pltpu.VMEM)] * 4,
        scratch_shapes=scratch + sems,
        compiler_params=pltpu.CompilerParams(
            collective_id=0, has_side_effects=True, vmem_limit_bytes=60 * 1024 * 1024),
    )(chosen, queries[0], keys[0], values[0], out_grad[0], proj)

    wide = jax.ShapeDtypeStruct((tokens, dn * dc), bf16)
    thin = jax.ShapeDtypeStruct((tokens, n * dh), bf16)
    out, q_grad, k_grad, v_grad, proj_grad = pl.pallas_call(
        functools.partial(place_kernel, n, dn, tokens // BLOCK),
        out_shape=(wide, thin, thin, thin, jax.ShapeDtypeStruct((dh, dc), f32)),
        in_specs=[smem] + [vmem] * 4,
        out_specs=[vmem] * 5,
    )(chosen, mixed, dq, dkv, weight_grad)
    return out[None], q_grad[None], k_grad[None], v_grad[None], proj_grad


def solution(mesh):
    rows = P("dp", "ctx", None)
    return jax.shard_map(
        shards,
        mesh=mesh,
        in_specs=(rows, rows, rows, rows, P("dp", None), P("ctx", "dp")),
        out_specs=(rows, rows, rows, rows, P("ctx", "dp")),
        check_vma=False,
    )
```

profile of v0, /device:TPU:0, one launch (start us, length us, event | category | flops | bytes accessed | tf_op | source)
XLA Modules:
  0.0 87.6 jit_solution(169175872633799859)
XLA Ops:
  0.6 83.7 %shard_map.101 = (bf16[8,128,128]{2,1,0:T(8,128)(2,1)}, bf16[8,2,128,128]{3,2,1,0:T(8,128)(2,1)}, f32[128,512]{1,0:T(8,128)}, bf16[4,128,512]{2,1,0:T(8,128)(2,1)}) custom-call(s32[1,8]{1,0:T(1,128)} %picked.3, bf16[256,1024]{1,0:T(8,128)(2,1)} %bitcast.9, bf16[256,1024]{1,0:T(8,128)(2,1)} %bitcast.10, bf16[256,1024]{1,0:T(8,128)(2,1)} %bitcast.11, ...), custom_call_target="tpu_custom_call" | custom-call | tf_op jit(solution)/shard_map/pallas_call | solution.py:341
  84.4 3.2 %shard_map.102 = (bf16[256,2048]{1,0:T(8,128)(2,1)}, bf16[256,1024]{1,0:T(8,128)(2,1)}, bf16[256,1024]{1,0:T(8,128)(2,1)}, bf16[256,1024]{1,0:T(8,128)(2,1)}, f32[128,512]{1,0:T(8,128)}) custom-call(s32[1,8]{1,0:T(1,128)} %picked.3, bf16[4,128,512]{2,1,0:T(8,128)(2,1)} %get-tuple-element.14.mix, bf16[8,128,128]{2,1,0:T(8,128)(2,1)} %get-tuple-element.15.dq, ...), custom_call_target="tpu_custom_call" | custom-call | tf_op jit(solution)/shard_map/pallas_call | solution.py:358
where the time goes:
time: 87.8 us; the launch traced here: 87.6 us
  Pallas kernels  87 us (99%)
    pallas_call x1, Pallas kernels, shards(): pl.pallas_call(functools.partial(kernel, n, dn, 1.0 / math.sqrt(dh)), out...  83.7 us
    pallas_call x1, Pallas kernels, shards(): pl.pallas_call(functools.partial(place_kernel, n, dn, tokens // BLOCK), o...  3.24 us

commit v1 on v0

v1 whole, which is shorter than its diff:
```python
import functools
import math

import jax
import jax.numpy as jnp
from jax import lax
from jax.experimental import pallas as pl
from jax.experimental.pallas import tpu as pltpu
from jax.sharding import PartitionSpec as P

BLOCK = 128
FAR = 1 << 30


def dot_nt(a, b):
    return lax.dot_general(a, b, (((1,), (1,)), ((), ())), preferred_element_type=jnp.float32)


def dot_nn(a, b):
    return lax.dot_general(a, b, (((1,), (0,)), ((), ())), preferred_element_type=jnp.float32)


def transposed(a):
    return a.astype(jnp.float32).T.astype(a.dtype)


def block_marks(picked, me, count):
    entry = picked[0, me]
    spans = count // 2
    index = jnp.maximum(entry, 0)
    local = jnp.where(index // spans == me, index % spans, spans + index % spans)
    local = jnp.where(entry >= 0, local, -1)
    return [jnp.where(local == j, 1.0, 0.0) for j in range(count)]


def place_kernel(
    n, dn, count, picked, mix, dq, dkv, w, out, q_out, k_out, v_out, w_out,
    mix_v, dq_v, dkv_v, out_v, q_v, k_v, v_v, in_s, out_s,
):
    loads = [
        pltpu.make_async_copy(mix, mix_v, in_s.at[0]),
        pltpu.make_async_copy(dq, dq_v, in_s.at[1]),
        pltpu.make_async_copy(dkv, dkv_v, in_s.at[2]),
    ]
    for copy in loads:
        copy.start()
    stores = [pltpu.make_async_copy(w, w_out, out_s.at[4])]
    stores[0].start()
    marks = block_marks(picked, lax.axis_index("ctx"), count)
    block, dh, dc = dq.shape[1], dq.shape[2], mix.shape[2]

    def spread(dst, cols, value):
        value = value.astype(jnp.float32)
        for j, mark in enumerate(marks):
            dst[j * block:(j + 1) * block, cols] = (value * mark).astype(dst.dtype)

    def put(src, dst, sem):
        copy = pltpu.make_async_copy(src, dst, sem)
        copy.start()
        stores.append(copy)

    loads[0].wait()
    for d in range(dn):
        spread(out_v, slice(d * dc, (d + 1) * dc), mix_v[d])
    put(out_v, out, out_s.at[0])
    loads[1].wait()
    for h in range(n):
        spread(q_v, slice(h * dh, (h + 1) * dh), dq_v[h])
    put(q_v, q_out, out_s.at[1])
    loads[2].wait()
    for t, (dst, ref) in enumerate(((k_v, k_out), (v_v, v_out))):
        for h in range(n):
            spread(dst, slice(h * dh, (h + 1) * dh), dkv_v[h, t])
        put(dst, ref, out_s.at[2 + t])
    for copy in stores:
        copy.wait()


scope = jax.named_scope


def kernel(
    n, dn, scale,
    picked, q_hbm, k_hbm, v_hbm, g_hbm, proj,
    dq_r, dkv_r, w_out, mix_r,
    q_in, k_in, v_in, g_in, qkv, g, kpos, qkv_r, g_r, proj_r, agp_s, agp_r, ag_s, ag_r, attn_s, attn_r, attn_d, attn_t,
    p_s, k_t, v_t, dq_s, dkv_s, dk_acc, dv_acc, w_s, w_y, w_x, w_m, w_p, mix_s,
    qkv_ss, qkv_rs, g_ss, g_rs, proj_ss, proj_rs, fwd_ss, pass_ss, agp_ss, agp_rs, ag_ss, ag_rs,
    attn_ss, attn_rs, ad_ss, ad_rs, ad_fs, dq_ss, dq_rs, dkv_ss, dkv_rs, w_ss, wy_rs, wx_rs, wm_rs, wp_rs, mix_ss, mix_rs,
    loc,
):
    me = lax.axis_index("ctx")
    md = lax.axis_index("dp")
    bf16 = jnp.bfloat16
    block, dh = qkv.shape[2], qkv.shape[3]
    dc = proj.shape[1]
    slots = n * block
    width = 2 * block
    rows = n // 2
    half = rows // 2

    def ctx_copy(src, dst, ss, rs, peer):
        return pltpu.make_async_remote_copy(
            src_ref=src, dst_ref=dst, send_sem=ss, recv_sem=rs,
            device_id={"ctx": peer}, device_id_type=pl.DeviceIdType.MESH)

    def dp_copy(src, dst, ss, rs, peer):
        return pltpu.make_async_remote_copy(
            src_ref=src, dst_ref=dst, send_sem=ss, recv_sem=rs,
            device_id={"dp": peer}, device_id_type=pl.DeviceIdType.MESH)

    ctx_peers = [lax.rem(me + s, n) for s in range(1, n)]
    dp_peers = [lax.rem(md + s, dn) for s in range(1, dn)]

    barrier = pltpu.get_barrier_semaphore()
    for peer in ctx_peers:
        pl.semaphore_signal(barrier, inc=1, device_id={"ctx": peer}, device_id_type=pl.DeviceIdType.MESH)
    for peer in dp_peers:
        pl.semaphore_signal(barrier, inc=1, device_id={"dp": peer}, device_id_type=pl.DeviceIdType.MESH)

    own_proj = pltpu.make_async_copy(proj, proj_r.at[me], loc.at[2])
    loads = [
        pltpu.make_async_copy(src, dst, loc.at[6 + t])
        for t, (src, dst) in enumerate(((g_hbm, g_in), (q_hbm, q_in), (k_hbm, k_in), (v_hbm, v_in)))]
    for copy in loads:
        copy.start()
    own_proj.start()
    marks = block_marks(picked, me, q_in.shape[0] // block)

    def chosen_rows(ref, low, high):
        total = None
        for j, mark in enumerate(marks):
            term = ref[j * block:(j + 1) * block, low:high].astype(jnp.float32) * mark
            total = term if total is None else total + term
        return total.astype(bf16)

    row = me // 2
    side = lax.rem(me, 2)
    pair = me + 1 - 2 * side
    own_base = (row // half) * half
    far_base = half - own_base

    def near(s):
        return own_base + lax.rem(row + s, half)

    def across(s):
        return far_base + lax.rem(row + s, half)

    mates = [near(s) for s in range(1, half)]
    partner = across(0)
    mate_partners = [across(s) for s in range(1, half)]

    with scope("A_load"):
        loads[0].wait()
        for j in range(dn):
            g[j] = chosen_rows(g_in, j * dc, (j + 1) * dc)
        g_r[md] = g[md]
        for t, ref in enumerate((q_in, k_in, v_in)):
            loads[1 + t].wait()
            for h in range(n):
                qkv[h, t] = chosen_rows(ref, h * dh, (h + 1) * dh)
        qkv_r[me] = qkv[me]
    with scope("B_barrier"):
        pl.semaphore_wait(barrier, n - 1 + dn - 1)
    sends = []

    def go(copy):
        copy.start()
        sends.append(copy)

    for a in [partner] + mates:
        peer = 2 * a + side
        go(ctx_copy(proj, proj_r.at[me], proj_ss.at[peer], proj_rs.at[me], peer))
    go(ctx_copy(proj, proj_r.at[me], proj_ss.at[pair], proj_rs.at[me], pair))
    for peer in dp_peers:
        go(dp_copy(g.at[peer], g_r.at[md], g_ss.at[peer], g_rs.at[md], peer))

    def send_qkv(peers):
        for peer in peers:
            go(ctx_copy(qkv.at[peer], qkv_r.at[me], qkv_ss.at[peer], qkv_rs.at[me], peer))

    far_heads = [2 * across(s) + (side if t == 0 else 1 - side) for s in range(half) for t in range(2)]
    near_heads = [2 * a + (side if t == 0 else 1 - side) for a in mates for t in range(2)] + [pair]
    early_far = len(far_heads) // 2
    send_qkv(far_heads[:early_far])

    down = lax.broadcasted_iota(jnp.int32, (block, block), 0)
    for j in range(n):
        entry = picked[0, j]
        kpos[j * block:(j + 1) * block] = down + jnp.where(entry >= 0, entry * block, FAR)

    def ctx_arrived(buf, ss, rs, peer):
        ctx_copy(buf.at[peer], buf.at[peer], ss.at[peer], rs.at[peer], peer).wait_recv()

    def dp_arrived(buf, ss, rs, peer):
        dp_copy(buf.at[peer], buf.at[peer], ss.at[peer], rs.at[peer], peer).wait_recv()

    def proj_arrived(h):
        ctx_arrived(proj_r, proj_ss, proj_rs, h)

    def pass_pair(h):
        go(ctx_copy(proj_r.at[h], proj_r.at[h], fwd_ss.at[h], proj_rs.at[h], pair))

    with scope("C_waitmate"):
        for a in mates:
            proj_arrived(2 * a + side)
            pass_pair(2 * a + side)
    with scope("D_waitpartner"):
        ph = 2 * partner + side
        proj_arrived(ph)
        for a in mates:
            peer = 2 * a + side
            go(ctx_copy(proj_r.at[ph], proj_r.at[ph], pass_ss.at[peer], proj_rs.at[ph], peer))
        pass_pair(ph)
    send_qkv(far_heads[early_far:] + near_heads)
    own_proj.wait()
    with scope("E_waitg"):
        for peer in dp_peers:
            dp_arrived(g_r, g_ss, g_rs, peer)

    def part(h):
        out = dot_nt(g_r[...].reshape(dn * block, dc), proj_r[h]).astype(bf16)
        agp_s[h] = out.reshape(dn, block, dh)
        for peer in dp_peers:
            go(dp_copy(agp_s.at[h, peer], agp_r.at[h, md], agp_ss.at[h, peer], agp_rs.at[h, md], peer))

    def finish(h):
        total = agp_s[h, md].astype(jnp.float32)
        for peer in dp_peers:
            dp_copy(agp_r.at[h, peer], agp_r.at[h, peer], agp_ss.at[h, peer], agp_rs.at[h, peer], peer).wait_recv()
            total = total + agp_r[h, peer].astype(jnp.float32)
        ag_s[h] = total.astype(bf16)
        if h is me:
            ag_r[me] = ag_s[me]
        else:
            go(ctx_copy(ag_s.at[h], ag_r.at[me], ag_ss.at[h], ag_rs.at[me], h))

    first = [2 * partner + side] + [2 * a + side for a in mates]
    second = [2 * a + side for a in mate_partners]
    cross = [2 * a + 1 - side for a in mates + [partner]]
    heads = [(h, False) for h in first] + [(me, False), (pair, True)]
    heads += [(h, True) for h in cross] + [(h, True) for h in second]
    heads += [(2 * a + 1 - side, True) for a in mate_partners]
    lag = 2
    for k, (h, pending) in enumerate(heads):
        if pending:
            with scope("F_waitproj"):
                proj_arrived(h)
        if any(h is other for other in second):
            pass_pair(h)
        with scope("G_part"):
            part(h)
        if k >= lag:
            with scope("H_finish"):
                finish(heads[k - lag][0])
    for h, _ in heads[-lag:]:
        with scope("H_finish"):
            finish(h)

    with scope("I_waitqkv"):
        for peer in ctx_peers:
            ctx_arrived(qkv_r, qkv_ss, qkv_rs, peer)
    k_t[...] = transposed(qkv_r[:, 1].reshape(slots, dh))
    v_t[...] = transposed(qkv_r[:, 2].reshape(slots, dh))

    def ordered(k):
        late = k // half
        return far_base * (1 - late) + own_base * late + lax.rem(row + k + late, half)

    def send_pair(i, src, dst, ss, rs, own_sem):
        for t in range(2):
            peer = 2 * i + t

            @pl.when(peer != me)
            def _():
                ctx_copy(src.at[peer], dst.at[me], ss.at[peer], rs.at[me], peer).start()

            @pl.when(peer == me)
            def _():
                pltpu.make_async_copy(src.at[peer], dst.at[peer], own_sem).start()

    def forward(k, carry):
        i = ordered(k)
        q = qkv_r[pl.ds(2 * i, 2), 0].reshape(width, dh)
        keys = qkv_r[:, 1].reshape(slots, dh)
        scores = dot_nt(keys, q) * scale
        key_pos = kpos[...]
        key_pos = jnp.concatenate([key_pos, key_pos], axis=1)
        same = lax.broadcasted_iota(jnp.int32, (slots, width), 0) == (
            lax.broadcasted_iota(jnp.int32, (slots, width), 1) + i * width)
        lane = lax.broadcasted_iota(jnp.int32, (1, width), 1)
        first, second = picked[0, 2 * i], picked[0, 2 * i + 1]
        first = jnp.where(first >= 0, first * block, -FAR)
        second = jnp.where(second >= 0, (second - 1) * block, -FAR)
        query_pos = lane + jnp.where(lane < block, first, second)
        scores = jnp.where((key_pos <= query_pos) | same, scores, -1e30)
        e = jnp.exp(scores - jnp.max(scores, axis=0, keepdims=True))
        p = (e * (1.0 / jnp.sum(e, axis=0, keepdims=True))).astype(bf16)
        p_s[i] = p
        a_t = dot_nn(v_t[...], p)
        attn_t[i] = a_t.astype(bf16)
        attn_s[pl.ds(2 * i, 2)] = a_t.T.astype(bf16).reshape(2, block, dh)
        send_pair(i, attn_s, attn_r, attn_ss, attn_rs, loc.at[3])
        return carry

    with scope("J_forward"):
        lax.fori_loop(0, rows, forward, 0)

    dk_acc[...] = jnp.zeros_like(dk_acc)
    dv_acc[...] = jnp.zeros_like(dv_acc)

    def backward(k, carry):
        i = ordered(k)
        with scope("K_waitag"):
            for t in range(2):
                peer = 2 * i + t

                @pl.when(peer != me)
                def _():
                    ctx_arrived(ag_r, ag_ss, ag_rs, peer)
        q = qkv_r[pl.ds(2 * i, 2), 0].reshape(width, dh)
        v = qkv_r[:, 2].reshape(slots, dh)
        da = ag_r[pl.ds(2 * i, 2)].reshape(width, dh)
        delta = jnp.sum(da.astype(jnp.float32).T * attn_t[i].astype(jnp.float32), axis=0, keepdims=True)
        p = p_s[i]
        ds = (p.astype(jnp.float32) * (dot_nt(v, da) - delta)).astype(bf16)
        dq_t = dot_nn(k_t[...], ds) * scale
        dq_s[pl.ds(2 * i, 2)] = dq_t.T.astype(bf16).reshape(2, block, dh)
        send_pair(i, dq_s, dq_r, dq_ss, dq_rs, loc.at[4])
        dk_acc[...] += dot_nn(ds, q)
        dv_acc[...] += dot_nn(p, da)
        return carry

    twin = md + 1 - 2 * lax.rem(md, 2)
    dp_far = [lax.rem(md + 2 * s, dn) for s in range(1, dn // 2)]
    groups = [pl.ds(2 * far_base, rows), pl.ds(2 * own_base, rows)]
    own_attn = []

    def spread_attn(t):
        part_of = groups[t]
        for peer in dp_far + [twin]:
            go(dp_copy(attn_r.at[part_of], attn_d.at[md, part_of], ad_ss.at[t, peer], ad_rs.at[t, md], peer))
        copy = pltpu.make_async_copy(attn_r.at[part_of], attn_d.at[md, part_of], loc.at[t])
        copy.start()
        own_attn.append(copy)

    def group_arrived(t, peer):
        view = attn_d.at[peer, groups[t]]
        dp_copy(view, view, ad_ss.at[t, peer], ad_rs.at[t, peer], peer).wait_recv()

    early = rows - 1
    with scope("L_backward"):
        lax.fori_loop(0, early, backward, 0)
    with scope("M_waitattn"):
        for h in far_heads:
            ctx_arrived(attn_r, attn_ss, attn_rs, h)
        spread_attn(0)
    with scope("L_backward"):
        lax.fori_loop(early, rows, backward, 0)

    dkv_s[:, 0] = (dk_acc[...] * scale).astype(bf16).reshape(n, block, dh)
    dkv_s[:, 1] = dv_acc[...].astype(bf16).reshape(n, block, dh)
    for peer in far_heads + near_heads:
        go(ctx_copy(dkv_s.at[peer], dkv_r.at[me], dkv_ss.at[peer], dkv_rs.at[me], peer))
    own_dkv = pltpu.make_async_copy(dkv_s.at[me], dkv_r.at[me], loc.at[5])
    own_dkv.start()

    with scope("M_waitattn"):
        for h in near_heads:
            ctx_arrived(attn_r, attn_ss, attn_rs, h)
        pltpu.make_async_copy(attn_s.at[me], attn_r.at[me], loc.at[3]).wait()
        spread_attn(1)

    with scope("N_waitspread"):
        for t in range(2):
            for peer in dp_far:
                group_arrived(t, peer)
                view = attn_d.at[peer, groups[t]]
                go(dp_copy(view, view, ad_fs.at[t, peer], ad_rs.at[t, peer], twin))
        for t in range(2):
            for peer in [twin] + [lax.rem(twin + 2 * s, dn) for s in range(1, dn // 2)]:
                group_arrived(t, peer)
        for copy in own_attn:
            copy.wait()

    def weight(h):
        heads_of = attn_d[:, h].reshape(dn * block, dh)
        return dot_nn(transposed(heads_of), g_r[...].reshape(dn * block, dc))

    orders = mate_partners + [partner] + mates + [row]
    with scope("P_weight"):
        for a in orders:
            h = 2 * a + 1 - side
            w_s[h] = weight(h).astype(bf16)
            go(ctx_copy(w_s.at[h], w_y.at[a], w_ss.at[h], wy_rs.at[a], pair))

    def mix_step(j, carry):
        rows_of = jnp.concatenate(
            [attn_d[pl.ds(2 * j, 2), h].reshape(width, dh) for h in range(n)], axis=1)
        out = dot_nn(rows_of, proj_r[...].reshape(n * dh, dc))
        mix_s[pl.ds(2 * j, 2)] = out.astype(bf16).reshape(2, block, dc)
        return carry

    with scope("Q_mix"):
        lax.fori_loop(0, dn // 2, mix_step, 0)
    for peer in dp_peers:
        go(dp_copy(mix_s.at[peer], mix_r.at[md], mix_ss.at[peer], mix_rs.at[md], peer))
    own_mix = pltpu.make_async_copy(mix_s.at[md], mix_r.at[md], loc.at[2])
    own_mix.start()

    def both_sides(a):
        total = weight(2 * a + side)
        with scope("R_waitside"):
            ctx_copy(w_y.at[a], w_y.at[a], w_ss.at[me], wy_rs.at[a], pair).wait_recv()
        return total + w_y[a].astype(jnp.float32)

    def send_w(a, total, dst, rs, peer_row):
        h = 2 * a + side
        w_s[h] = total.astype(bf16)
        go(ctx_copy(w_s.at[h], dst, w_ss.at[h], rs, 2 * peer_row + side))

    for a, mate in zip(mate_partners, mates):
        send_w(a, both_sides(a), w_x.at[row], wx_rs.at[row], mate)
    total = both_sides(partner)
    with scope("S_waitcross"):
        for a in mates:
            ctx_copy(w_x.at[a], w_x.at[a], w_ss.at[me], wx_rs.at[a], pair).wait_recv()
            total = total + w_x[a].astype(jnp.float32)
    send_w(partner, total, w_p, wp_rs.at[0], partner)
    for a in mates:
        send_w(a, both_sides(a), w_m.at[row], wm_rs.at[row], a)
    w_out[...] = both_sides(row)

    with scope("T_waitdq"):
        pltpu.make_async_copy(dq_s.at[me], dq_r.at[me], loc.at[4]).wait()
        for peer in ctx_peers:
            ctx_arrived(dq_r, dq_ss, dq_rs, peer)
    with scope("U_waitdkv"):
        own_dkv.wait()
        for peer in ctx_peers:
            ctx_arrived(dkv_r, dkv_ss, dkv_rs, peer)
    with scope("V_waitmix"):
        own_mix.wait()
        for peer in dp_peers:
            dp_arrived(mix_r, mix_ss, mix_rs, peer)
    with scope("W_waitmates"):
        for a in mates:
            ctx_copy(w_m.at[a], w_m.at[a], w_ss.at[me], wm_rs.at[a], pair).wait_recv()
            w_out[...] += w_m[a].astype(jnp.float32)
    with scope("X_waitpartner"):
        ctx_copy(w_p, w_p, w_ss.at[me], wp_rs.at[0], pair).wait_recv()
        w_out[...] += w_p[...].astype(jnp.float32)

    with scope("Y_waitsend"):
        for copy in sends:
            copy.wait_send()
        for peer in ctx_peers:
            ctx_copy(attn_s.at[peer], attn_r.at[me], attn_ss.at[peer], attn_rs.at[me], peer).wait_send()
            ctx_copy(dq_s.at[peer], dq_r.at[me], dq_ss.at[peer], dq_rs.at[me], peer).wait_send()


def shards(queries, keys, values, out_grad, chosen, proj):
    n = lax.axis_size("ctx")
    dn = lax.axis_size("dp")
    tokens = queries.shape[1]
    hd = queries.shape[2]
    dh = hd // n
    dc = proj.shape[1]
    slots = n * BLOCK
    width = 2 * BLOCK
    rows = n // 2
    bf16, f32 = jnp.bfloat16, jnp.float32
    sem = pltpu.SemaphoreType.DMA
    vm = pltpu.VMEM
    blocks = (n, BLOCK, dh)
    sheets = (rows, dh, dc)
    scratch = [
        vm((tokens, hd), bf16), vm((tokens, hd), bf16), vm((tokens, hd), bf16), vm((tokens, dn * dc), bf16),
        vm((n, 3, BLOCK, dh), bf16), vm((dn, BLOCK, dc), bf16), vm((slots, BLOCK), jnp.int32),
        vm((n, 3, BLOCK, dh), bf16), vm((dn, BLOCK, dc), bf16), vm((n, dh, dc), bf16),
        vm((n, dn, BLOCK, dh), bf16), vm((n, dn, BLOCK, dh), bf16), vm(blocks, bf16), vm(blocks, bf16),
        vm(blocks, bf16), vm(blocks, bf16), vm((dn,) + blocks, bf16), vm((rows, dh, width), bf16),
        vm((rows, slots, width), bf16), vm((dh, slots), bf16), vm((dh, slots), bf16),
        vm(blocks, bf16), vm((n, 2, BLOCK, dh), bf16), vm((slots, dh), f32), vm((slots, dh), f32),
        vm((n, dh, dc), bf16), vm(sheets, bf16), vm(sheets, bf16), vm(sheets, bf16), vm((dh, dc), bf16),
        vm((dn, BLOCK, dc), bf16),
    ]
    c, d = sem((n,)), sem((dn,))
    e = sem((n, dn))
    f = sem((2, dn))
    sems = [
        c, c, d, d, c, c, c, c, e, e, c, c,
        c, c, f, f, f, c, c, c, c, c, c, c, c, sem((1,)), d, d,
        sem((10,)),
    ]
    vmem = pl.BlockSpec(memory_space=pltpu.VMEM)
    smem = pl.BlockSpec(memory_space=pltpu.SMEM)
    hbm = pl.BlockSpec(memory_space=pl.ANY)
    dq, dkv, weight_grad, mixed = pl.pallas_call(
        functools.partial(kernel, n, dn, 1.0 / math.sqrt(dh)),
        out_shape=(
            jax.ShapeDtypeStruct(blocks, bf16),
            jax.ShapeDtypeStruct((n, 2, BLOCK, dh), bf16),
            jax.ShapeDtypeStruct((dh, dc), f32),
            jax.ShapeDtypeStruct((dn, BLOCK, dc), bf16),
        ),
        in_specs=[smem] + [hbm] * 5,
        out_specs=[hbm, hbm, vmem, hbm],
        scratch_shapes=scratch + sems,
        compiler_params=pltpu.CompilerParams(
            collective_id=0, has_side_effects=True, vmem_limit_bytes=60 * 1024 * 1024),
    )(chosen, queries[0], keys[0], values[0], out_grad[0], proj)

    wide = (tokens, dn * dc)
    thin = (tokens, hd)
    out, q_grad, k_grad, v_grad, proj_grad = pl.pallas_call(
        functools.partial(place_kernel, n, dn, tokens // BLOCK),
        out_shape=(
            jax.ShapeDtypeStruct(wide, bf16), jax.ShapeDtypeStruct(thin, bf16), jax.ShapeDtypeStruct(thin, bf16),
            jax.ShapeDtypeStruct(thin, bf16), jax.ShapeDtypeStruct((dh, dc), f32)),
        in_specs=[smem] + [hbm] * 3 + [vmem],
        out_specs=[hbm] * 5,
        scratch_shapes=[
            vm((dn, BLOCK, dc), bf16), vm(blocks, bf16), vm((n, 2, BLOCK, dh), bf16),
            vm(wide, bf16), vm(thin, bf16), vm(thin, bf16), vm(thin, bf16), sem((3,)), sem((5,))],
    )(chosen, mixed, dq, dkv, weight_grad)
    return out[None], q_grad[None], k_grad[None], v_grad[None], proj_grad


def solution(mesh):
    rows = P("dp", "ctx", None)
    return jax.shard_map(
        shards,
        mesh=mesh,
        in_specs=(rows, rows, rows, rows, P("dp", None), P("ctx", "dp")),
        out_specs=(rows, rows, rows, rows, P("ctx", "dp")),
        check_vma=False,
    )
```

time: 87.8 us -> 86.3 us (0.983)
  Pallas kernels: 87 us -> 85.1 us
    pallas_call x1, Pallas kernels: 83.7 us -> 81.3 us  [shards(): pl.pallas_call(functools.partial(kernel, n, dn, 1.0 / math.sqrt(dh)), out...]
where the time goes in v1:
time: 86.3 us; the launch traced here: 85.7 us
  Pallas kernels  85.1 us (99%)
    pallas_call x1, Pallas kernels, shards(): pl.pallas_call(functools.partial(kernel, n, dn, 1.0 / math.sqrt(dh)), out...  81.3 us
    pallas_call x1, Pallas kernels, shards(): pl.pallas_call(functools.partial(place_kernel, n, dn, tokens // BLOCK), o...  3.79 us

profile of v1, /device:TPU:0, one launch (start us, length us, event | category | flops | bytes accessed | tf_op | source)
XLA Modules:
  0.0 85.7 jit_solution(17727172678547789405)
XLA Ops:
  0.6 81.3 %shard_map.101 = (bf16[8,128,128]{2,1,0:T(8,128)(2,1)}, bf16[8,2,128,128]{3,2,1,0:T(8,128)(2,1)}, f32[128,512]{1,0:T(8,128)}, bf16[4,128,512]{2,1,0:T(8,128)(2,1)}) custom-call(s32[1,8]{1,0:T(1,128)} %picked.3, bf16[256,1024]{1,0:T(8,128)(2,1)} %bitcast.9, bf16[256,1024]{1,0:T(8,128)(2,1)} %bitcast.10, bf16[256,1024]{1,0:T(8,128)(2,1)} %bitcast.11, ...), custom_call_target="tpu_custom_call" | custom-call | tf_op jit(solution)/shard_map/pallas_call | solution.py:499
  81.9 3.8 %shard_map.102 = (bf16[256,2048]{1,0:T(8,128)(2,1)}, bf16[256,1024]{1,0:T(8,128)(2,1)}, bf16[256,1024]{1,0:T(8,128)(2,1)}, bf16[256,1024]{1,0:T(8,128)(2,1)}, f32[128,512]{1,0:T(8,128)}) custom-call(s32[1,8]{1,0:T(1,128)} %picked.3, bf16[4,128,512]{2,1,0:T(8,128)(2,1)} %get-tuple-element.14.mix, bf16[8,128,128]{2,1,0:T(8,128)(2,1)} %get-tuple-element.15.dq, ...), custom_call_target="tpu_custom_call" | custom-call | tf_op jit(solution)/shard_map/pallas_call | solution.py:516

commit v2 on v0

v2 whole, which is shorter than its diff:
```python
import functools
import math

import jax
import jax.numpy as jnp
from jax import lax
from jax.experimental import pallas as pl
from jax.experimental.pallas import tpu as pltpu
from jax.sharding import PartitionSpec as P

BLOCK = 128
FAR = 1 << 30
MIB = 1024 * 1024
SPARE = 8 * MIB

scope = jax.named_scope


def dot_nt(a, b):
    return lax.dot_general(a, b, (((1,), (1,)), ((), ())), preferred_element_type=jnp.float32)


def dot_nn(a, b):
    return lax.dot_general(a, b, (((1,), (0,)), ((), ())), preferred_element_type=jnp.float32)


def transposed(a):
    return a.astype(jnp.float32).T.astype(a.dtype)


def local_block(picked, me, count):
    entry = picked[0, me]
    spans = count // 2
    index = jnp.maximum(entry, 0)
    local = jnp.where(index // spans == me, index % spans, spans + index % spans)
    return entry, local


def block_marks(picked, me, count):
    entry, local = local_block(picked, me, count)
    local = jnp.where(entry >= 0, local, -1)
    return [jnp.where(local == j, 1.0, 0.0) for j in range(count)]


def place_kernel(n, dn, count, picked, mix, dq, dkv, w, out, q_out, k_out, v_out, w_out, zero, sems, w_sem):
    block, dh, dc = dq.shape[1], dq.shape[2], mix.shape[2]
    entry, local = local_block(picked, lax.axis_index("ctx"), count)
    local = jnp.where(entry >= 0, local, -1)
    w_copy = pltpu.make_async_copy(w, w_out, w_sem.at[0])
    w_copy.start()
    zero[...] = jnp.zeros_like(zero)
    outs = (out, q_out, k_out, v_out)
    for j in range(count):
        rows = pl.ds(j * block, block)

        @pl.when(local == j)
        def _():
            for d in range(dn):
                pltpu.make_async_copy(mix.at[d], out.at[rows, pl.ds(d * dc, dc)], sems.at[j, 0]).start()
            for h in range(n):
                cols = pl.ds(h * dh, dh)
                pltpu.make_async_copy(dq.at[h], q_out.at[rows, cols], sems.at[j, 1]).start()
                pltpu.make_async_copy(dkv.at[h, 0], k_out.at[rows, cols], sems.at[j, 2]).start()
                pltpu.make_async_copy(dkv.at[h, 1], v_out.at[rows, cols], sems.at[j, 3]).start()

        @pl.when(local != j)
        def _():
            for t, dst in enumerate(outs):
                pltpu.make_async_copy(zero.at[:, pl.ds(0, dst.shape[1])], dst.at[rows], sems.at[j, t]).start()

    for j in range(count):
        for t, dst in enumerate(outs):
            view = dst.at[pl.ds(j * block, block)]
            pltpu.make_async_copy(view, view, sems.at[j, t]).wait()
    w_copy.wait()


def kernel(
    n, dn, scale,
    picked, q_hbm, k_hbm, v_hbm, g_hbm, proj,
    dq_r, dkv_r, w_out, mix_r,
    qkv_in, g_in, qkv, g, kpos, qkv_r, g_r, proj_r, agp_s, agp_r, ag_s, ag_r,
    attn_s, attn_r, attn_y, attn_d, attn_e, attn_t,
    p_s, k_t, v_t, dq_s, dkv_s, dk_acc, dv_acc, w_s, w_x, w_m, w_p, mix_s,
    ss, rs, proj_rs, agp_rs, ag_rs, ad_rs, ae_rs, loc,
):
    me = lax.axis_index("ctx")
    md = lax.axis_index("dp")
    bf16 = jnp.bfloat16
    block, dh = qkv.shape[2], qkv.shape[3]
    dc = proj.shape[1]
    slots = n * block
    width = 2 * block
    rows = n // 2
    half = rows // 2
    s_proj, s_g, s_qkv, s_agp, s_ag, s_gp, s_attn, s_dq, s_dkv, s_ad, s_ap, s_ae, s_w, s_mix, s_pass = (
        ss.at[k] for k in range(15))
    r_g, r_qkv, r_gp, r_attn0, r_attn1, r_dq, r_dkv, r_ap, r_wx, r_wm, r_wp, r_mix = (rs.at[k] for k in range(12))

    def ctx_copy(src, dst, send, recv, peer):
        return pltpu.make_async_remote_copy(
            src_ref=src, dst_ref=dst, send_sem=send, recv_sem=recv,
            device_id={"ctx": peer}, device_id_type=pl.DeviceIdType.MESH)

    def dp_copy(src, dst, send, recv, peer):
        return pltpu.make_async_remote_copy(
            src_ref=src, dst_ref=dst, send_sem=send, recv_sem=recv,
            device_id={"dp": peer}, device_id_type=pl.DeviceIdType.MESH)

    ctx_peers = [lax.rem(me + s, n) for s in range(1, n)]
    dp_peers = [lax.rem(md + s, dn) for s in range(1, dn)]

    barrier = pltpu.get_barrier_semaphore()
    for peer in ctx_peers:
        pl.semaphore_signal(barrier, inc=1, device_id={"ctx": peer}, device_id_type=pl.DeviceIdType.MESH)
    for peer in dp_peers:
        pl.semaphore_signal(barrier, inc=1, device_id={"dp": peer}, device_id_type=pl.DeviceIdType.MESH)

    row = me // 2
    side = lax.rem(me, 2)
    other = 1 - side
    pair = me + 1 - 2 * side
    own_base = (row // half) * half
    far_base = half - own_base

    def near(s):
        return own_base + lax.rem(row + s, half)

    def across(s):
        return far_base + lax.rem(row + s, half)

    mates = [near(s) for s in range(1, half)]
    partner = across(0)
    mate_partners = [across(s) for s in range(1, half)]

    own_proj = pltpu.make_async_copy(proj, proj_r.at[side, row], loc.at[0])
    g_load = pltpu.make_async_copy(g_hbm, g_in, loc.at[1])
    g_load.start()
    for t, src in enumerate((q_hbm, k_hbm, v_hbm)):
        pltpu.make_async_copy(src, qkv_in.at[t], loc.at[2]).start()
    own_proj.start()
    marks = block_marks(picked, me, qkv_in.shape[1] // block)

    def chosen_rows(load):
        total = None
        for j, mark in enumerate(marks):
            term = load(slice(j * block, (j + 1) * block)).astype(jnp.float32) * mark
            total = term if total is None else total + term
        return total.astype(bf16)

    def arrived(view, recv):
        ctx_copy(view, view, s_proj, recv, pair).wait_recv()

    def sent(view, send):
        ctx_copy(view, view, send, r_g, pair).wait_send()

    with scope("A_load"):
        g_load.wait()
        for j in range(dn):
            g[j] = chosen_rows(lambda r: g_in[r, j * dc:(j + 1) * dc])
        g_r[side, md] = g[md]
        pltpu.make_async_copy(qkv_in, qkv_in, loc.at[2]).wait()
        for t in range(3):
            for h in range(n):
                qkv[h, t] = chosen_rows(lambda r: qkv_in[t, r, h * dh:(h + 1) * dh])
        qkv_r[me] = qkv[me]
    with scope("B_barrier"):
        pl.semaphore_wait(barrier, n - 1 + dn - 1)

    own_block = proj_r.at[side, row]
    for peer in [2 * a + side for a in [partner] + mates] + [pair]:
        ctx_copy(proj, own_block, s_proj, proj_rs.at[side, row], peer).start()
    for peer in dp_peers:
        dp_copy(g.at[peer], g_r.at[side, md], s_g, r_g, peer).start()

    def send_qkv(peers):
        for peer in peers:
            ctx_copy(qkv.at[peer], qkv_r.at[me], s_qkv, r_qkv, peer).start()

    send_qkv([2 * a + side for a in [partner] + mate_partners])

    down = lax.broadcasted_iota(jnp.int32, (block, block), 0)
    for j in range(n):
        entry = picked[0, j]
        kpos[j * block:(j + 1) * block] = down + jnp.where(entry >= 0, entry * block, FAR)

    def proj_arrived(a, s):
        arrived(proj_r.at[s, a], proj_rs.at[s, a])

    def pass_on(a, peer):
        ctx_copy(proj_r.at[side, a], proj_r.at[side, a], s_pass, proj_rs.at[side, a], peer).start()

    with scope("C_waitmate"):
        for a in mates:
            proj_arrived(a, side)
            pass_on(a, pair)
    with scope("D_waitpartner"):
        proj_arrived(partner, side)
        for a in mates:
            pass_on(partner, 2 * a + side)
        pass_on(partner, pair)
    send_qkv([2 * a + side for a in mates])
    own_proj.wait()
    with scope("E_waitg"):
        arrived(g_r.at[side, pl.ds(0, dn - 1)], r_g)

    def part(a, s):
        h = 2 * a + s
        out = dot_nt(g_r[side].reshape(dn * block, dc), proj_r[s, a]).astype(bf16)
        agp_s[h] = out.reshape(dn, block, dh)
        for peer in dp_peers:
            dp_copy(agp_s.at[h, peer], agp_r.at[h, md], s_agp, agp_rs.at[h], peer).start()

    def finish(a, s):
        h = 2 * a + s
        arrived(agp_r.at[h, pl.ds(0, dn - 1)], agp_rs.at[h])
        total = agp_s[h, md].astype(jnp.float32)
        for peer in dp_peers:
            total = total + agp_r[h, peer].astype(jnp.float32)
        if a is row and s is side:
            ag_r[me] = total.astype(bf16)
        else:
            ag_s[h] = total.astype(bf16)
            ctx_copy(ag_s.at[h], ag_r.at[me], s_ag, ag_rs.at[row], h).start()

    with scope("G_part"):
        first = [(partner, side)] + [(a, side) for a in mates] + [(row, side)]
        for a, s in first:
            part(a, s)
    with scope("F_waitsecond"):
        for a in mate_partners:
            proj_arrived(a, side)
            pass_on(a, pair)
    send_qkv([2 * a + other for a in [partner] + mate_partners + mates] + [pair])
    rest = [(a, side) for a in mate_partners]
    rest += [(row, other)] + [(a, other) for a in mates + [partner] + mate_partners]
    waiting = first
    for a, s in rest:
        if s is other:
            with scope("F_waitproj"):
                proj_arrived(a, s)
        with scope("G_part"):
            part(a, s)
        with scope("H_finish"):
            finish(*waiting[0])
        waiting = waiting[1:] + [(a, s)]
    with scope("H_finish"):
        for a, s in waiting:
            finish(a, s)
    ctx_copy(g_r.at[side], g_r.at[side], s_gp, r_gp, pair).start()

    with scope("I_waitqkv"):
        arrived(qkv_r.at[pl.ds(0, n - 1)], r_qkv)
    k_t[...] = transposed(qkv_r[:, 1].reshape(slots, dh))
    v_t[...] = transposed(qkv_r[:, 2].reshape(slots, dh))

    def ordered(k):
        late = k // half
        return far_base * (1 - late) + own_base * late + lax.rem(row + k + late, half)

    def forward(k, carry):
        i = ordered(k)
        q = qkv_r[pl.ds(2 * i, 2), 0].reshape(width, dh)
        keys = qkv_r[:, 1].reshape(slots, dh)
        scores = dot_nt(keys, q) * scale
        key_pos = kpos[...]
        key_pos = jnp.concatenate([key_pos, key_pos], axis=1)
        same = lax.broadcasted_iota(jnp.int32, (slots, width), 0) == (
            lax.broadcasted_iota(jnp.int32, (slots, width), 1) + i * width)
        lane = lax.broadcasted_iota(jnp.int32, (1, width), 1)
        one, two = picked[0, 2 * i], picked[0, 2 * i + 1]
        one = jnp.where(one >= 0, one * block, -FAR)
        two = jnp.where(two >= 0, (two - 1) * block, -FAR)
        query_pos = lane + jnp.where(lane < block, one, two)
        scores = jnp.where((key_pos <= query_pos) | same, scores, -1e30)
        e = jnp.exp(scores - jnp.max(scores, axis=0, keepdims=True))
        p = (e * (1.0 / jnp.sum(e, axis=0, keepdims=True))).astype(bf16)
        p_s[i] = p
        a_t = dot_nn(v_t[...], p)
        attn_t[i] = a_t.astype(bf16)
        attn_s[i] = a_t.T.astype(bf16)

        @pl.when(k < half)
        def _():
            ctx_copy(attn_s.at[i], attn_r.at[row], s_attn, r_attn0, 2 * i + side).start()

        @pl.when((k >= half) & (k < rows - 1))
        def _():
            ctx_copy(attn_s.at[i], attn_r.at[row], s_attn, r_attn1, 2 * i + side).start()

        @pl.when(k == rows - 1)
        def _():
            pltpu.make_async_copy(attn_s.at[i], attn_r.at[i], loc.at[3]).start()

        return carry

    with scope("J_forward"):
        lax.fori_loop(0, rows, forward, 0)

    dk_acc[...] = jnp.zeros_like(dk_acc)
    dv_acc[...] = jnp.zeros_like(dv_acc)

    def backward(k, carry):
        i = ordered(k)
        with scope("K_waitag"):
            @pl.when(k < rows - 1)
            def _():
                arrived(ag_r.at[pl.ds(2 * i, 2)], ag_rs.at[i])

            @pl.when(k == rows - 1)
            def _():
                arrived(ag_r.at[pair], ag_rs.at[row])

        q = qkv_r[pl.ds(2 * i, 2), 0].reshape(width, dh)
        v = qkv_r[:, 2].reshape(slots, dh)
        da = ag_r[pl.ds(2 * i, 2)].reshape(width, dh)
        delta = jnp.sum(da.astype(jnp.float32).T * attn_t[i].astype(jnp.float32), axis=0, keepdims=True)
        p = p_s[i]
        ds = (p.astype(jnp.float32) * (dot_nt(v, da) - delta)).astype(bf16)
        dq_t = dot_nn(k_t[...], ds) * scale
        dq_s[pl.ds(2 * i, 2)] = dq_t.T.astype(bf16).reshape(2, block, dh)
        for t in range(2):
            peer = 2 * i + t

            @pl.when(peer != me)
            def _():
                ctx_copy(dq_s.at[peer], dq_r.at[me], s_dq, r_dq, peer).start()

            @pl.when(peer == me)
            def _():
                pltpu.make_async_copy(dq_s.at[peer], dq_r.at[peer], loc.at[4]).start()

        dk_acc[...] += dot_nn(ds, q)
        dv_acc[...] += dot_nn(p, da)
        return carry

    with scope("L_backward"):
        lax.fori_loop(0, rows, backward, 0)

    dkv_s[:, 0] = (dk_acc[...] * scale).astype(bf16).reshape(n, block, dh)
    dkv_s[:, 1] = dv_acc[...].astype(bf16).reshape(n, block, dh)
    for peer in [2 * a + s for a in [partner] + mate_partners + mates for s in (side, other)] + [pair]:
        ctx_copy(dkv_s.at[peer], dkv_r.at[me], s_dkv, r_dkv, peer).start()
    own_dkv = pltpu.make_async_copy(dkv_s.at[me], dkv_r.at[me], loc.at[5])
    own_dkv.start()

    twin = md + 1 - 2 * lax.rem(md, 2)
    dp_far = [lax.rem(md + 2 * s, dn) for s in range(1, dn // 2)]

    def spread(src, dst_of, send, recv, own_sem):
        for s, peer in enumerate(dp_far):
            dp_copy(src, dst_of(md), send, recv.at[1 + s], peer).start()
        dp_copy(src, dst_of(md), send, recv.at[0], twin).start()
        copy = pltpu.make_async_copy(src, dst_of(md), own_sem)
        copy.start()
        return copy

    def hand_over(dst_of, send, recv):
        for s in range(1, dn // 2):
            peer = lax.rem(md + dn - 2 * s, dn)
            arrived(dst_of(peer), recv.at[s])
            dp_copy(dst_of(peer), dst_of(peer), send, recv.at[0], twin).start()

    groups = [pl.ds(far_base, half), pl.ds(own_base, half)]
    with scope("M_waitattn"):
        arrived(attn_r.at[groups[0]], r_attn0)
    own_far = spread(attn_r.at[groups[0]], lambda d: attn_d.at[0, d, pl.ds(0, half)], s_ad, ad_rs.at[0], loc.at[6])
    with scope("M_waitattn"):
        if half > 1:
            arrived(attn_r.at[pl.ds(0, half - 1)], r_attn1)
        pltpu.make_async_copy(attn_s.at[row], attn_r.at[row], loc.at[3]).wait()
    own_near = spread(attn_r.at[groups[1]], lambda d: attn_d.at[1, d, pl.ds(0, half)], s_ad, ad_rs.at[1], loc.at[7])
    ctx_copy(attn_r.at[:, pl.ds(pl.multiple_of(other * block, block), block)], attn_y, s_ap, r_ap, pair).start()
    with scope("N_handover0"):
        hand_over(lambda d: attn_d.at[0, d, pl.ds(0, half)], s_ad, ad_rs.at[0])
    with scope("N_waitpair"):
        arrived(attn_y, r_ap)
    own_ae = spread(attn_y, lambda d: attn_e.at[d], s_ae, ae_rs, loc.at[8])
    with scope("N_handover1"):
        hand_over(lambda d: attn_d.at[1, d, pl.ds(0, half)], s_ad, ad_rs.at[1])
    with scope("N_waitspread"):
        own_far.wait()
        own_near.wait()
        for t in range(2):
            arrived(attn_d.at[t, pl.ds(0, dn // 2)], ad_rs.at[t, 0])
        arrived(g_r.at[other], r_gp)

    def weight(t, a):
        total = None
        for b in range(2):
            heads_of = attn_d[t, :, lax.rem(a, half), b * block:(b + 1) * block].reshape(dn * block, dh)
            term = dot_nn(transposed(heads_of), g_r[b].reshape(dn * block, dc))
            total = term if total is None else total + term
        return total

    def send_w(slot, value, dst, recv, peer_row):
        w_s[slot] = value.astype(bf16)
        ctx_copy(w_s.at[slot], dst, s_w, recv, 2 * peer_row + side).start()

    with scope("P_weight"):
        for k, a in enumerate(mate_partners):
            send_w(k, weight(0, a), w_x.at[row], r_wx, mates[k])
        crossing = weight(0, partner)
        for k, a in enumerate(mates):
            send_w(half - 1 + k, weight(1, a), w_m.at[row], r_wm, a)
        w_out[...] = weight(1, row)

    def cross_sum(total):
        if mates:
            arrived(w_x.at[pl.ds(0, half - 1)], r_wx)
        for a in mates:
            total = total + w_x[a].astype(jnp.float32)
        send_w(rows - 2, total, w_p, r_wp, partner)

    with scope("O_handover"):
        hand_over(lambda d: attn_e.at[d], s_ae, ae_rs)
        own_ae.wait()
        arrived(attn_e.at[pl.ds(0, dn // 2)], ae_rs.at[0])

    mine = pl.ds(pl.multiple_of(side * block, block), block)

    def mix_step(j, carry):
        def two(ref, *at):
            return ref[at].reshape(width, dh)

        d = pl.ds(2 * j, 2)
        t_of = [row // half if a // half else 1 - row // half for a in range(rows)]
        here = jnp.concatenate([two(attn_d, t_of[a], d, a % half, mine) for a in range(rows)], axis=1)
        there = jnp.concatenate([two(attn_e, d, a) for a in range(rows)], axis=1)
        out = dot_nn(here, proj_r[side].reshape(rows * dh, dc)) + dot_nn(there, proj_r[other].reshape(rows * dh, dc))
        mix_s[d] = out.astype(bf16).reshape(2, block, dc)
        return carry

    with scope("Q_mix"):
        lax.fori_loop(0, dn // 2, mix_step, 0)
    for peer in dp_peers:
        dp_copy(mix_s.at[peer], mix_r.at[md], s_mix, r_mix, peer).start()
    own_mix = pltpu.make_async_copy(mix_s.at[md], mix_r.at[md], loc.at[9])
    own_mix.start()

    with scope("S_waitcross"):
        cross_sum(crossing)

    with scope("T_waitdq"):
        pltpu.make_async_copy(dq_s.at[me], dq_r.at[me], loc.at[4]).wait()
        arrived(dq_r.at[pl.ds(0, n - 1)], r_dq)
    with scope("U_waitdkv"):
        own_dkv.wait()
        arrived(dkv_r.at[pl.ds(0, n - 1)], r_dkv)
    with scope("W_waitmates"):
        if mates:
            arrived(w_m.at[pl.ds(0, half - 1)], r_wm)
        for a in mates:
            w_out[...] += w_m[a].astype(jnp.float32)
    with scope("X_waitpartner"):
        arrived(w_p, r_wp)
        w_out[...] += w_p[...].astype(jnp.float32)
    with scope("V_waitmix"):
        own_mix.wait()
        arrived(mix_r.at[pl.ds(0, dn - 1)], r_mix)

    with scope("Y_waitsend"):
        blocks = pl.ds(0, n - 1)
        others = pl.ds(0, dn - 1)
        sent(qkv_r.at[pl.ds(0, n - 1)], s_qkv)
        sent(proj_r.at[0, pl.ds(0, half + 1)], s_proj)
        passed = rows + half - 2
        sent(proj_r.at[:, pl.ds(0, passed // 2)] if passed % 2 == 0 else proj_r.at[0, pl.ds(0, passed)], s_pass)
        sent(g.at[others], s_g)
        sent(agp_s.at[:, others], s_agp)
        sent(ag_s.at[blocks], s_ag)
        sent(g_r.at[0], s_gp)
        sent(attn_s.at[pl.ds(0, rows - 1)], s_attn)
        sent(dq_s.at[blocks], s_dq)
        sent(dkv_s.at[blocks], s_dkv)
        sent(attn_d.at[:, others], s_ad)
        sent(attn_y, s_ap)
        sent(attn_e.at[others], s_ae)
        sent(w_s.at[pl.ds(0, rows - 1)], s_w)
        sent(mix_s.at[others], s_mix)


def shards(queries, keys, values, out_grad, chosen, proj):
    n = lax.axis_size("ctx")
    dn = lax.axis_size("dp")
    tokens = queries.shape[1]
    hd = queries.shape[2]
    dh = hd // n
    dc = proj.shape[1]
    slots = n * BLOCK
    width = 2 * BLOCK
    rows = n // 2
    half = rows // 2
    bf16, f32 = jnp.bfloat16, jnp.float32
    sem = pltpu.SemaphoreType.DMA
    blocks = (n, BLOCK, dh)
    pairs = (rows, width, dh)
    sheets = (rows, dh, dc)
    buffers = [
        ((3, tokens, hd), bf16), ((tokens, dn * dc), bf16), ((n, 3, BLOCK, dh), bf16), ((dn, BLOCK, dc), bf16),
        ((slots, BLOCK), jnp.int32), ((n, 3, BLOCK, dh), bf16), ((2, dn, BLOCK, dc), bf16), ((2,) + sheets, bf16),
        ((n, dn, BLOCK, dh), bf16), ((n, dn, BLOCK, dh), bf16), (blocks, bf16), (blocks, bf16),
        (pairs, bf16), (pairs, bf16), ((rows, BLOCK, dh), bf16), ((2, dn, half, width, dh), bf16),
        ((dn, rows, BLOCK, dh), bf16), ((rows, dh, width), bf16),
        ((rows, slots, width), bf16), ((dh, slots), bf16), ((dh, slots), bf16),
        (blocks, bf16), ((n, 2, BLOCK, dh), bf16), ((slots, dh), f32), ((slots, dh), f32),
        (sheets, bf16), (sheets, bf16), (sheets, bf16), ((dh, dc), bf16), ((dn, BLOCK, dc), bf16),
    ]
    held = sum(math.prod(shape) * jnp.dtype(kind).itemsize for shape, kind in buffers)
    sems = [sem((15,)), sem((12,)), sem((2, rows)), sem((n,)), sem((rows,)), sem((2, dn // 2)), sem((dn // 2,)), sem((10,))]
    vmem = pl.BlockSpec(memory_space=pltpu.VMEM)
    smem = pl.BlockSpec(memory_space=pltpu.SMEM)
    free = pl.BlockSpec(memory_space=pl.ANY)
    hbm = pl.BlockSpec(memory_space=pltpu.HBM)
    dq, dkv, weight_grad, mixed = pl.pallas_call(
        functools.partial(kernel, n, dn, 1.0 / math.sqrt(dh)),
        out_shape=(
            jax.ShapeDtypeStruct(blocks, bf16),
            jax.ShapeDtypeStruct((n, 2, BLOCK, dh), bf16),
            jax.ShapeDtypeStruct((dh, dc), f32),
            jax.ShapeDtypeStruct((dn, BLOCK, dc), bf16),
        ),
        in_specs=[smem] + [hbm] * 5,
        out_specs=[free, free, vmem, free],
        scratch_shapes=[pltpu.VMEM(shape, kind) for shape, kind in buffers] + sems,
        compiler_params=pltpu.CompilerParams(
            collective_id=0, has_side_effects=True, vmem_limit_bytes=min(held + SPARE, 60 * MIB)),
    )(chosen, *[pltpu.with_memory_space_constraint(x, pltpu.HBM) for x in (queries[0], keys[0], values[0], out_grad[0], proj)])

    wide = (tokens, dn * dc)
    thin = (tokens, hd)
    count = tokens // BLOCK
    out, q_grad, k_grad, v_grad, proj_grad = pl.pallas_call(
        functools.partial(place_kernel, n, dn, count),
        out_shape=(
            jax.ShapeDtypeStruct(wide, bf16), jax.ShapeDtypeStruct(thin, bf16), jax.ShapeDtypeStruct(thin, bf16),
            jax.ShapeDtypeStruct(thin, bf16), jax.ShapeDtypeStruct((dh, dc), f32)),
        in_specs=[smem] + [free] * 4,
        out_specs=[hbm] * 5,
        scratch_shapes=[pltpu.VMEM((BLOCK, max(dn * dc, hd)), bf16), sem((count, 4)), sem((1,))],
        compiler_params=pltpu.CompilerParams(vmem_limit_bytes=8 * MIB),
    )(chosen, mixed, dq, dkv, weight_grad)
    return out[None], q_grad[None], k_grad[None], v_grad[None], proj_grad


def solution(mesh):
    rows = P("dp", "ctx", None)
    return jax.shard_map(
        shards,
        mesh=mesh,
        in_specs=(rows, rows, rows, rows, P("dp", None), P("ctx", "dp")),
        out_specs=(rows, rows, rows, rows, P("ctx", "dp")),
        check_vma=False,
    )
```

time: 87.8 us -> 79.8 us (0.909)
  Pallas kernels: 87 us -> 78.3 us
    pallas_call x1, Pallas kernels: 83.7 us -> 76.1 us  [shards(): pl.pallas_call(functools.partial(kernel, n, dn, 1.0 / math.sqrt(dh)), out...]
    pallas_call x1, Pallas kernels: 3.24 us -> 2.18 us  [shards(): pl.pallas_call(functools.partial(place_kernel, n, dn, count), out_shape=(...]
where the time goes in v2:
time: 79.8 us; the launch traced here: 79.6 us
  Pallas kernels  78.3 us (98%)
    pallas_call x1, Pallas kernels, shards(): pl.pallas_call(functools.partial(kernel, n, dn, 1.0 / math.sqrt(dh)), out...  76.1 us
    pallas_call x1, Pallas kernels, shards(): pl.pallas_call(functools.partial(place_kernel, n, dn, count), out_shape=(...  2.18 us

profile of v2, /device:TPU:0, one launch (start us, length us, event | category | flops | bytes accessed | tf_op | source)
XLA Modules:
  0.0 79.6 jit_solution(5482317204763973624)
XLA Ops:
  0.6 0.0 copy-start
  0.6 0.6 copy-done
  1.3 76.1 %shard_map.101 = (bf16[8,128,128]{2,1,0:T(8,128)(2,1)S(1)}, bf16[8,2,128,128]{3,2,1,0:T(8,128)(2,1)S(1)}, f32[128,512]{1,0:T(8,128)S(1)}, bf16[4,128,512]{2,1,0:T(8,128)(2,1)S(1)}) custom-call(s32[1,8]{1,0:T(1,128)S(1)} %copy-done, bf16[256,1024]{1,0:T(8,128)(2,1)} %bitcast.9, bf16[256,1024]{1,0:T(8,128)(2,1)} %bitcast.10, bf16[256,1024]{1,0:T(8,128)(2,1)} %bitcast.11, ...), custom_call_target="tpu_custom_call" | custom-call | tf_op jit(solution)/shard_map/pallas_call | solution.py:515
  77.4 2.2 %shard_map.102 = (bf16[256,2048]{1,0:T(8,128)(2,1)}, bf16[256,1024]{1,0:T(8,128)(2,1)}, bf16[256,1024]{1,0:T(8,128)(2,1)}, bf16[256,1024]{1,0:T(8,128)(2,1)}, f32[128,512]{1,0:T(8,128)}) custom-call(s32[1,8]{1,0:T(1,128)S(1)} %copy-done, bf16[4,128,512]{2,1,0:T(8,128)(2,1)S(1)} %get-tuple-element.14.mix, bf16[8,128,128]{2,1,0:T(8,128)(2,1)S(1)} %get-tuple-element.15.dq, ...), custom_call_target="tpu_custom_call" | custom-call | tf_op jit(solution)/shard_map/pallas_call | solution.py:533
Async XLA Ops:
  0.6 0.7 copy-start

commit v3 on v2

--- a/solution.py
+++ b/solution.py
@@ -42,13 +42,16 @@
     return [jnp.where(local == j, 1.0, 0.0) for j in range(count)]
 
 
-def place_kernel(n, dn, count, picked, mix, dq, dkv, w, out, q_out, k_out, v_out, w_out, zero, sems, w_sem):
+def place_kernel(n, dn, count, chosen, mix, dq, dkv, w, out, q_out, k_out, v_out, w_out, picked, zero, sems, w_sem):
     block, dh, dc = dq.shape[1], dq.shape[2], mix.shape[2]
-    entry, local = local_block(picked, lax.axis_index("ctx"), count)
-    local = jnp.where(entry >= 0, local, -1)
+    pick = pltpu.make_async_copy(chosen, picked, w_sem.at[1])
+    pick.start()
     w_copy = pltpu.make_async_copy(w, w_out, w_sem.at[0])
     w_copy.start()
     zero[...] = jnp.zeros_like(zero)
+    pick.wait()
+    entry, local = local_block(picked, lax.axis_index("ctx"), count)
+    local = jnp.where(entry >= 0, local, -1)
     outs = (out, q_out, k_out, v_out)
     for j in range(count):
         rows = pl.ds(j * block, block)
@@ -77,9 +80,9 @@
 
 def kernel(
     n, dn, scale,
-    picked, q_hbm, k_hbm, v_hbm, g_hbm, proj,
+    chosen, q_hbm, k_hbm, v_hbm, g_hbm, proj,
     dq_r, dkv_r, w_out, mix_r,
-    qkv_in, g_in, qkv, g, kpos, qkv_r, g_r, proj_r, agp_s, agp_r, ag_s, ag_r,
+    picked, qkv_in, g_in, qkv, g, kpos, qkv_r, g_r, proj_r, agp_s, agp_r, ag_s, ag_r,
     attn_s, attn_r, attn_y, attn_d, attn_e, attn_t,
     p_s, k_t, v_t, dq_s, dkv_s, dk_acc, dv_acc, w_s, w_x, w_m, w_p, mix_s,
     ss, rs, proj_rs, agp_rs, ag_rs, ad_rs, ae_rs, loc,
@@ -133,12 +136,15 @@
     partner = across(0)
     mate_partners = [across(s) for s in range(1, half)]
 
+    pick = pltpu.make_async_copy(chosen, picked, loc.at[10])
+    pick.start()
     own_proj = pltpu.make_async_copy(proj, proj_r.at[side, row], loc.at[0])
     g_load = pltpu.make_async_copy(g_hbm, g_in, loc.at[1])
     g_load.start()
     for t, src in enumerate((q_hbm, k_hbm, v_hbm)):
         pltpu.make_async_copy(src, qkv_in.at[t], loc.at[2]).start()
     own_proj.start()
+    pick.wait()
     marks = block_marks(picked, me, qkv_in.shape[1] // block)
 
     def chosen_rows(load):
@@ -233,7 +239,8 @@
             pass_on(a, pair)
     send_qkv([2 * a + other for a in [partner] + mate_partners + mates] + [pair])
     rest = [(a, side) for a in mate_partners]
-    rest += [(row, other)] + [(a, other) for a in mates + [partner] + mate_partners]
+    rest += [(row, other)] + [(a, other) for a in mates + [partner]]
+    last = [(a, other) for a in mate_partners]
     waiting = first
     for a, s in rest:
         if s is other:
@@ -295,7 +302,17 @@
         return carry
 
     with scope("J_forward"):
-        lax.fori_loop(0, rows, forward, 0)
+        lax.fori_loop(0, half, forward, 0)
+    for a, s in last:
+        with scope("F_waitproj"):
+            proj_arrived(a, s)
+        with scope("G_part"):
+            part(a, s)
+    with scope("J_forward"):
+        lax.fori_loop(half, rows, forward, 0)
+    for a, s in last:
+        with scope("H_finish"):
+            finish(a, s)
 
     dk_acc[...] = jnp.zeros_like(dk_acc)
     dv_acc[...] = jnp.zeros_like(dv_acc)
@@ -339,8 +356,12 @@
 
     dkv_s[:, 0] = (dk_acc[...] * scale).astype(bf16).reshape(n, block, dh)
     dkv_s[:, 1] = dv_acc[...].astype(bf16).reshape(n, block, dh)
-    for peer in [2 * a + s for a in [partner] + mate_partners + mates for s in (side, other)] + [pair]:
-        ctx_copy(dkv_s.at[peer], dkv_r.at[me], s_dkv, r_dkv, peer).start()
+
+    def send_dkv(peers):
+        for peer in peers:
+            ctx_copy(dkv_s.at[peer], dkv_r.at[me], s_dkv, r_dkv, peer).start()
+
+    send_dkv([2 * a + side for a in [partner] + mate_partners + mates])
     own_dkv = pltpu.make_async_copy(dkv_s.at[me], dkv_r.at[me], loc.at[5])
     own_dkv.start()
 
@@ -371,11 +392,9 @@
         pltpu.make_async_copy(attn_s.at[row], attn_r.at[row], loc.at[3]).wait()
     own_near = spread(attn_r.at[groups[1]], lambda d: attn_d.at[1, d, pl.ds(0, half)], s_ad, ad_rs.at[1], loc.at[7])
     ctx_copy(attn_r.at[:, pl.ds(pl.multiple_of(other * block, block), block)], attn_y, s_ap, r_ap, pair).start()
+    send_dkv([2 * a + other for a in [partner] + mate_partners + mates] + [pair])
     with scope("N_handover0"):
         hand_over(lambda d: attn_d.at[0, d, pl.ds(0, half)], s_ad, ad_rs.at[0])
-    with scope("N_waitpair"):
-        arrived(attn_y, r_ap)
-    own_ae = spread(attn_y, lambda d: attn_e.at[d], s_ae, ae_rs, loc.at[8])
     with scope("N_handover1"):
         hand_over(lambda d: attn_d.at[1, d, pl.ds(0, half)], s_ad, ad_rs.at[1])
     with scope("N_waitspread"):
@@ -404,6 +423,10 @@
         for k, a in enumerate(mates):
             send_w(half - 1 + k, weight(1, a), w_m.at[row], r_wm, a)
         w_out[...] = weight(1, row)
+
+    with scope("N_waitpair"):
+        arrived(attn_y, r_ap)
+    own_ae = spread(attn_y, lambda d: attn_e.at[d], s_ae, ae_rs, loc.at[8])
 
     def cross_sum(total):
         if mates:
@@ -507,11 +530,16 @@
         (sheets, bf16), (sheets, bf16), (sheets, bf16), ((dh, dc), bf16), ((dn, BLOCK, dc), bf16),
     ]
     held = sum(math.prod(shape) * jnp.dtype(kind).itemsize for shape, kind in buffers)
-    sems = [sem((15,)), sem((12,)), sem((2, rows)), sem((n,)), sem((rows,)), sem((2, dn // 2)), sem((dn // 2,)), sem((10,))]
+    sems = [sem((15,)), sem((12,)), sem((2, rows)), sem((n,)), sem((rows,)), sem((2, dn // 2)), sem((dn // 2,)), sem((11,))]
     vmem = pl.BlockSpec(memory_space=pltpu.VMEM)
-    smem = pl.BlockSpec(memory_space=pltpu.SMEM)
+    picks = pltpu.SMEM(chosen.shape, chosen.dtype)
     free = pl.BlockSpec(memory_space=pl.ANY)
     hbm = pl.BlockSpec(memory_space=pltpu.HBM)
+
+    def kept(x):
+        return pltpu.with_memory_space_constraint(x, pltpu.HBM)
+
+    chosen = kept(chosen)
     dq, dkv, weight_grad, mixed = pl.pallas_call(
         functools.partial(kernel, n, dn, 1.0 / math.sqrt(dh)),
         out_shape=(
@@ -520,12 +548,12 @@
             jax.ShapeDtypeStruct((dh, dc), f32),
             jax.ShapeDtypeStruct((dn, BLOCK, dc), bf16),
         ),
-        in_specs=[smem] + [hbm] * 5,
+        in_specs=[hbm] * 6,
         out_specs=[free, free, vmem, free],
-        scratch_shapes=[pltpu.VMEM(shape, kind) for shape, kind in buffers] + sems,
+        scratch_shapes=[picks] + [pltpu.VMEM(shape, kind) for shape, kind in buffers] + sems,
         compiler_params=pltpu.CompilerParams(
             collective_id=0, has_side_effects=True, vmem_limit_bytes=min(held + SPARE, 60 * MIB)),
-    )(chosen, *[pltpu.with_memory_space_constraint(x, pltpu.HBM) for x in (queries[0], keys[0], values[0], out_grad[0], proj)])
+    )(chosen, *[kept(x) for x in (queries[0], keys[0], values[0], out_grad[0], proj)])
 
     wide = (tokens, dn * dc)
     thin = (tokens, hd)
@@ -535,9 +563,9 @@
         out_shape=(
             jax.ShapeDtypeStruct(wide, bf16), jax.ShapeDtypeStruct(thin, bf16), jax.ShapeDtypeStruct(thin, bf16),
             jax.ShapeDtypeStruct(thin, bf16), jax.ShapeDtypeStruct((dh, dc), f32)),
-        in_specs=[smem] + [free] * 4,
+        in_specs=[hbm] + [free] * 4,
         out_specs=[hbm] * 5,
-        scratch_shapes=[pltpu.VMEM((BLOCK, max(dn * dc, hd)), bf16), sem((count, 4)), sem((1,))],
+        scratch_shapes=[picks, pltpu.VMEM((BLOCK, max(dn * dc, hd)), bf16), sem((count, 4)), sem((2,))],
         compiler_params=pltpu.CompilerParams(vmem_limit_bytes=8 * MIB),
     )(chosen, mixed, dq, dkv, weight_grad)
     return out[None], q_grad[None], k_grad[None], v_grad[None], proj_grad

time: 79.8 us -> 75.8 us (0.950)
  Pallas kernels: 78.3 us -> 75 us
    pallas_call x1, Pallas kernels: 76.1 us -> 72.7 us  [shards(): pl.pallas_call(functools.partial(kernel, n, dn, 1.0 / math.sqrt(dh)), out...]
where the time goes in v3:
time: 75.8 us; the launch traced here: 75.6 us
  Pallas kernels  75 us (99%)
    pallas_call x1, Pallas kernels, shards(): pl.pallas_call(functools.partial(kernel, n, dn, 1.0 / math.sqrt(dh)), out...  72.7 us
    pallas_call x1, Pallas kernels, shards(): pl.pallas_call(functools.partial(place_kernel, n, dn, count), out_shape=(...  2.25 us

profile of v3, /device:TPU:0, one launch (start us, length us, event | category | flops | bytes accessed | tf_op | source)
XLA Modules:
  0.0 75.6 jit_solution(8088957291370273259)
XLA Ops:
  0.6 72.7 %shard_map.101 = (bf16[8,128,128]{2,1,0:T(8,128)(2,1)S(1)}, bf16[8,2,128,128]{3,2,1,0:T(8,128)(2,1)S(1)}, f32[128,512]{1,0:T(8,128)S(1)}, bf16[4,128,512]{2,1,0:T(8,128)(2,1)S(1)}) custom-call(s32[1,8]{1,0:T(1,128)} %chosen.3, bf16[256,1024]{1,0:T(8,128)(2,1)} %bitcast.9, bf16[256,1024]{1,0:T(8,128)(2,1)} %bitcast.10, bf16[256,1024]{1,0:T(8,128)(2,1)} %bitcast.11, ...), custom_call_target="tpu_custom_call" | custom-call | tf_op jit(solution)/shard_map/pallas_call | solution.py:543
  73.4 2.3 %shard_map.102 = (bf16[256,2048]{1,0:T(8,128)(2,1)}, bf16[256,1024]{1,0:T(8,128)(2,1)}, bf16[256,1024]{1,0:T(8,128)(2,1)}, bf16[256,1024]{1,0:T(8,128)(2,1)}, f32[128,512]{1,0:T(8,128)}) custom-call(s32[1,8]{1,0:T(1,128)} %chosen.3, bf16[4,128,512]{2,1,0:T(8,128)(2,1)S(1)} %get-tuple-element.14.mix, bf16[8,128,128]{2,1,0:T(8,128)(2,1)S(1)} %get-tuple-element.15.dq, ...), custom_call_target="tpu_custom_call" | custom-call | tf_op jit(solution)/shard_map/pallas_call | solution.py:561

commit v4 on v3

--- a/solution.py
+++ b/solution.py
@@ -85,7 +85,7 @@
     picked, qkv_in, g_in, qkv, g, kpos, qkv_r, g_r, proj_r, agp_s, agp_r, ag_s, ag_r,
     attn_s, attn_r, attn_y, attn_d, attn_e, attn_t,
     p_s, k_t, v_t, dq_s, dkv_s, dk_acc, dv_acc, w_s, w_x, w_m, w_p, mix_s,
-    ss, rs, proj_rs, agp_rs, ag_rs, ad_rs, ae_rs, loc,
+    ss, rs, proj_rs, g_rs, agp_rs, ag_rs, ad_rs, ae_rs, loc,
 ):
     me = lax.axis_index("ctx")
     md = lax.axis_index("dp")
@@ -96,9 +96,9 @@
     width = 2 * block
     rows = n // 2
     half = rows // 2
-    s_proj, s_g, s_qkv, s_agp, s_ag, s_gp, s_attn, s_dq, s_dkv, s_ad, s_ap, s_ae, s_w, s_mix, s_pass = (
-        ss.at[k] for k in range(15))
-    r_g, r_qkv, r_gp, r_attn0, r_attn1, r_dq, r_dkv, r_ap, r_wx, r_wm, r_wp, r_mix = (rs.at[k] for k in range(12))
+    s_proj, s_g, s_qkv, s_agp, s_ag, s_gp, s_attn, s_dq, s_dkv, s_ad, s_ap, s_ae, s_w, s_mix, s_pass, s_pp = (
+        ss.at[k] for k in range(16))
+    r_pp, r_qkv, r_gp, r_attn0, r_attn1, r_dq, r_dkv, r_ap, r_wx, r_wm, r_wp, r_mix = (rs.at[k] for k in range(12))
 
     def ctx_copy(src, dst, send, recv, peer):
         return pltpu.make_async_remote_copy(
@@ -158,7 +158,7 @@
         ctx_copy(view, view, s_proj, recv, pair).wait_recv()
 
     def sent(view, send):
-        ctx_copy(view, view, send, r_g, pair).wait_send()
+        ctx_copy(view, view, send, r_pp, pair).wait_send()
 
     with scope("A_load"):
         g_load.wait()
@@ -173,11 +173,16 @@
     with scope("B_barrier"):
         pl.semaphore_wait(barrier, n - 1 + dn - 1)
 
+    twin = md + 1 - 2 * lax.rem(md, 2)
+    dp_far = [lax.rem(md + 2 * s, dn) for s in range(1, dn // 2)]
+    dp_cross = [lax.rem(twin + 2 * s, dn) for s in range(1, dn // 2)]
+
     own_block = proj_r.at[side, row]
-    for peer in [2 * a + side for a in [partner] + mates] + [pair]:
-        ctx_copy(proj, own_block, s_proj, proj_rs.at[side, row], peer).start()
-    for peer in dp_peers:
-        dp_copy(g.at[peer], g_r.at[side, md], s_g, r_g, peer).start()
+    for a in [partner] + mates:
+        ctx_copy(proj, own_block, s_proj, proj_rs.at[row], 2 * a + side).start()
+    for peer in dp_far + dp_cross + [twin]:
+        dp_copy(g.at[peer], g_r.at[side, md], s_g, g_rs.at[md], peer).start()
+    ctx_copy(g.at[md], g_r.at[side, md], s_gp, r_gp, pair).start()
 
     def send_qkv(peers):
         for peer in peers:
@@ -190,71 +195,67 @@
         entry = picked[0, j]
         kpos[j * block:(j + 1) * block] = down + jnp.where(entry >= 0, entry * block, FAR)
 
-    def proj_arrived(a, s):
-        arrived(proj_r.at[s, a], proj_rs.at[s, a])
-
-    def pass_on(a, peer):
-        ctx_copy(proj_r.at[side, a], proj_r.at[side, a], s_pass, proj_rs.at[side, a], peer).start()
-
-    with scope("C_waitmate"):
+    def proj_arrived(a):
+        arrived(proj_r.at[side, a], proj_rs.at[a])
+
+    with scope("C_waitg"):
+        for peer in [twin] + dp_far + dp_cross:
+            view = g_r.at[side, peer]
+            arrived(view, g_rs.at[peer])
+            ctx_copy(view, view, s_gp, r_gp, pair).start()
+    with scope("D_waitpartner"):
+        proj_arrived(partner)
+        view = proj_r.at[side, partner]
         for a in mates:
-            proj_arrived(a, side)
-            pass_on(a, pair)
-    with scope("D_waitpartner"):
-        proj_arrived(partner, side)
+            ctx_copy(view, view, s_pass, proj_rs.at[partner], 2 * a + side).start()
+    send_qkv([2 * a + other for a in [partner] + mate_partners])
+    send_qkv([2 * a + s for a in mates for s in (side, other)] + [pair])
+    own_proj.wait()
+
+    def part(a, b):
+        k = 2 * a + b
+        out = dot_nt(g_r[b].reshape(dn * block, dc), proj_r[side, a]).astype(bf16)
+        agp_s[k] = out.reshape(dn, block, dh)
+        for peer in dp_far + dp_cross + [twin]:
+            dp_copy(agp_s.at[k, peer], agp_r.at[k, md], s_agp, agp_rs.at[k], peer).start()
+
+    def finish(a, b):
+        k = 2 * a + b
+        arrived(agp_r.at[k, pl.ds(0, dn - 1)], agp_rs.at[k])
+        total = agp_s[k, md].astype(jnp.float32)
+        for peer in dp_peers:
+            total = total + agp_r[k, peer].astype(jnp.float32)
+        if a is row:
+            ag_r[2 * row + b] = total.astype(bf16)
+        else:
+            ag_s[k] = total.astype(bf16)
+            ctx_copy(ag_s.at[k], ag_r.at[2 * row + b], s_ag, ag_rs.at[row], 2 * a + side).start()
+
+    def parts(names, b, waiting, lag):
+        for a in names:
+            with scope("G_part"):
+                part(a, b)
+            waiting.append((a, b))
+            if len(waiting) > lag:
+                with scope("H_finish"):
+                    finish(*waiting.pop(0))
+
+    waiting = []
+    with scope("E_waitmate"):
         for a in mates:
-            pass_on(partner, 2 * a + side)
-        pass_on(partner, pair)
-    send_qkv([2 * a + side for a in mates])
-    own_proj.wait()
-    with scope("E_waitg"):
-        arrived(g_r.at[side, pl.ds(0, dn - 1)], r_g)
-
-    def part(a, s):
-        h = 2 * a + s
-        out = dot_nt(g_r[side].reshape(dn * block, dc), proj_r[s, a]).astype(bf16)
-        agp_s[h] = out.reshape(dn, block, dh)
-        for peer in dp_peers:
-            dp_copy(agp_s.at[h, peer], agp_r.at[h, md], s_agp, agp_rs.at[h], peer).start()
-
-    def finish(a, s):
-        h = 2 * a + s
-        arrived(agp_r.at[h, pl.ds(0, dn - 1)], agp_rs.at[h])
-        total = agp_s[h, md].astype(jnp.float32)
-        for peer in dp_peers:
-            total = total + agp_r[h, peer].astype(jnp.float32)
-        if a is row and s is side:
-            ag_r[me] = total.astype(bf16)
-        else:
-            ag_s[h] = total.astype(bf16)
-            ctx_copy(ag_s.at[h], ag_r.at[me], s_ag, ag_rs.at[row], h).start()
-
-    with scope("G_part"):
-        first = [(partner, side)] + [(a, side) for a in mates] + [(row, side)]
-        for a, s in first:
-            part(a, s)
+            proj_arrived(a)
+    parts([partner] + mates + [row], side, waiting, n)
     with scope("F_waitsecond"):
         for a in mate_partners:
-            proj_arrived(a, side)
-            pass_on(a, pair)
-    send_qkv([2 * a + other for a in [partner] + mate_partners + mates] + [pair])
-    rest = [(a, side) for a in mate_partners]
-    rest += [(row, other)] + [(a, other) for a in mates + [partner]]
-    last = [(a, other) for a in mate_partners]
-    waiting = first
-    for a, s in rest:
-        if s is other:
-            with scope("F_waitproj"):
-                proj_arrived(a, s)
-        with scope("G_part"):
-            part(a, s)
-        with scope("H_finish"):
-            finish(*waiting[0])
-        waiting = waiting[1:] + [(a, s)]
+            proj_arrived(a)
+    parts(mate_partners, side, waiting, n)
+    with scope("F_waitpairg"):
+        arrived(g_r.at[other], r_gp)
+    parts([partner] + mate_partners + mates + [row], other, waiting, rows)
     with scope("H_finish"):
-        for a, s in waiting:
-            finish(a, s)
-    ctx_copy(g_r.at[side], g_r.at[side], s_gp, r_gp, pair).start()
+        for a, b in waiting:
+            finish(a, b)
+    ctx_copy(proj_r.at[side], proj_r.at[side], s_pp, r_pp, pair).start()
 
     with scope("I_waitqkv"):
         arrived(qkv_r.at[pl.ds(0, n - 1)], r_qkv)
@@ -302,17 +303,7 @@
         return carry
 
     with scope("J_forward"):
-        lax.fori_loop(0, half, forward, 0)
-    for a, s in last:
-        with scope("F_waitproj"):
-            proj_arrived(a, s)
-        with scope("G_part"):
-            part(a, s)
-    with scope("J_forward"):
-        lax.fori_loop(half, rows, forward, 0)
-    for a, s in last:
-        with scope("H_finish"):
-            finish(a, s)
+        lax.fori_loop(0, rows, forward, 0)
 
     dk_acc[...] = jnp.zeros_like(dk_acc)
     dv_acc[...] = jnp.zeros_like(dv_acc)
@@ -323,10 +314,6 @@
             @pl.when(k < rows - 1)
             def _():
                 arrived(ag_r.at[pl.ds(2 * i, 2)], ag_rs.at[i])
-
-            @pl.when(k == rows - 1)
-            def _():
-                arrived(ag_r.at[pair], ag_rs.at[row])
 
         q = qkv_r[pl.ds(2 * i, 2), 0].reshape(width, dh)
         v = qkv_r[:, 2].reshape(slots, dh)
@@ -364,9 +351,6 @@
     send_dkv([2 * a + side for a in [partner] + mate_partners + mates])
     own_dkv = pltpu.make_async_copy(dkv_s.at[me], dkv_r.at[me], loc.at[5])
     own_dkv.start()
-
-    twin = md + 1 - 2 * lax.rem(md, 2)
-    dp_far = [lax.rem(md + 2 * s, dn) for s in range(1, dn // 2)]
 
     def spread(src, dst_of, send, recv, own_sem):
         for s, peer in enumerate(dp_far):
@@ -395,6 +379,9 @@
     send_dkv([2 * a + other for a in [partner] + mate_partners + mates] + [pair])
     with scope("N_handover0"):
         hand_over(lambda d: attn_d.at[0, d, pl.ds(0, half)], s_ad, ad_rs.at[0])
+    with scope("N_waitpair"):
+        arrived(attn_y, r_ap)
+    own_ae = spread(attn_y, lambda d: attn_e.at[d], s_ae, ae_rs, loc.at[8])
     with scope("N_handover1"):
         hand_over(lambda d: attn_d.at[1, d, pl.ds(0, half)], s_ad, ad_rs.at[1])
     with scope("N_waitspread"):
@@ -402,7 +389,6 @@
         own_near.wait()
         for t in range(2):
             arrived(attn_d.at[t, pl.ds(0, dn // 2)], ad_rs.at[t, 0])
-        arrived(g_r.at[other], r_gp)
 
     def weight(t, a):
         total = None
@@ -424,9 +410,6 @@
             send_w(half - 1 + k, weight(1, a), w_m.at[row], r_wm, a)
         w_out[...] = weight(1, row)
 
-    with scope("N_waitpair"):
-        arrived(attn_y, r_ap)
-    own_ae = spread(attn_y, lambda d: attn_e.at[d], s_ae, ae_rs, loc.at[8])
 
     def cross_sum(total):
         if mates:
@@ -437,6 +420,10 @@
 
     with scope("O_handover"):
         hand_over(lambda d: attn_e.at[d], s_ae, ae_rs)
+    with scope("S_waitcross"):
+        cross_sum(crossing)
+    with scope("O_waitrows"):
+        arrived(proj_r.at[other], r_pp)
         own_ae.wait()
         arrived(attn_e.at[pl.ds(0, dn // 2)], ae_rs.at[0])
 
@@ -460,9 +447,6 @@
         dp_copy(mix_s.at[peer], mix_r.at[md], s_mix, r_mix, peer).start()
     own_mix = pltpu.make_async_copy(mix_s.at[md], mix_r.at[md], loc.at[9])
     own_mix.start()
-
-    with scope("S_waitcross"):
-        cross_sum(crossing)
 
     with scope("T_waitdq"):
         pltpu.make_async_copy(dq_s.at[me], dq_r.at[me], loc.at[4]).wait()
@@ -486,12 +470,13 @@
         blocks = pl.ds(0, n - 1)
         others = pl.ds(0, dn - 1)
         sent(qkv_r.at[pl.ds(0, n - 1)], s_qkv)
-        sent(proj_r.at[0, pl.ds(0, half + 1)], s_proj)
-        passed = rows + half - 2
-        sent(proj_r.at[:, pl.ds(0, passed // 2)] if passed % 2 == 0 else proj_r.at[0, pl.ds(0, passed)], s_pass)
+        sent(proj_r.at[0, pl.ds(0, half)], s_proj)
+        if mates:
+            sent(proj_r.at[0, pl.ds(0, half - 1)], s_pass)
+        sent(proj_r.at[0], s_pp)
         sent(g.at[others], s_g)
         sent(agp_s.at[:, others], s_agp)
-        sent(ag_s.at[blocks], s_ag)
+        sent(ag_s.at[pl.ds(0, n - 2)], s_ag)
         sent(g_r.at[0], s_gp)
         sent(attn_s.at[pl.ds(0, rows - 1)], s_attn)
         sent(dq_s.at[blocks], s_dq)
@@ -530,7 +515,7 @@
         (sheets, bf16), (sheets, bf16), (sheets, bf16), ((dh, dc), bf16), ((dn, BLOCK, dc), bf16),
     ]
     held = sum(math.prod(shape) * jnp.dtype(kind).itemsize for shape, kind in buffers)
-    sems = [sem((15,)), sem((12,)), sem((2, rows)), sem((n,)), sem((rows,)), sem((2, dn // 2)), sem((dn // 2,)), sem((11,))]
+    sems = [sem((16,)), sem((12,)), sem((rows,)), sem((dn,)), sem((n,)), sem((rows,)), sem((2, dn // 2)), sem((dn // 2,)), sem((11,))]
     vmem = pl.BlockSpec(memory_space=pltpu.VMEM)
     picks = pltpu.SMEM(chosen.shape, chosen.dtype)
     free = pl.BlockSpec(memory_space=pl.ANY)

time: 75.8 us -> 72.8 us (0.960)
  the two profiles are of different devices: /device:TPU:0 before, /device:TPU:25 now
where the time goes in v4:
time: 72.8 us; the launch traced here: 72.6 us
  Pallas kernels  71.9 us (99%)
    pallas_call x1, Pallas kernels, shards(): pl.pallas_call(functools.partial(kernel, n, dn, 1.0 / math.sqrt(dh)), out...  69.7 us
    pallas_call x1, Pallas kernels, shards(): pl.pallas_call(functools.partial(place_kernel, n, dn, count), out_shape=(...  2.23 us

profile of v4, /device:TPU:25, one launch (start us, length us, event | category | flops | bytes accessed | tf_op | source)
XLA Modules:
  0.0 72.6 jit_solution(11392920757972995559)
XLA Ops:
  0.6 69.7 %shard_map.101 = (bf16[8,128,128]{2,1,0:T(8,128)(2,1)S(1)}, bf16[8,2,128,128]{3,2,1,0:T(8,128)(2,1)S(1)}, f32[128,512]{1,0:T(8,128)S(1)}, bf16[4,128,512]{2,1,0:T(8,128)(2,1)S(1)}) custom-call(s32[1,8]{1,0:T(1,128)} %chosen.3, bf16[256,1024]{1,0:T(8,128)(2,1)} %bitcast.9, bf16[256,1024]{1,0:T(8,128)(2,1)} %bitcast.10, bf16[256,1024]{1,0:T(8,128)(2,1)} %bitcast.11, ...), custom_call_target="tpu_custom_call" | custom-call | tf_op jit(solution)/shard_map/pallas_call | solution.py:528
  70.3 2.2 %shard_map.102 = (bf16[256,2048]{1,0:T(8,128)(2,1)}, bf16[256,1024]{1,0:T(8,128)(2,1)}, bf16[256,1024]{1,0:T(8,128)(2,1)}, bf16[256,1024]{1,0:T(8,128)(2,1)}, f32[128,512]{1,0:T(8,128)}) custom-call(s32[1,8]{1,0:T(1,128)} %chosen.3, bf16[4,128,512]{2,1,0:T(8,128)(2,1)S(1)} %get-tuple-element.14.mix, bf16[8,128,128]{2,1,0:T(8,128)(2,1)S(1)} %get-tuple-element.15.dq, ...), custom_call_target="tpu_custom_call" | custom-call | tf_op jit(solution)/shard_map/pallas_call | solution.py:546

commit v5 on v4

--- a/solution.py
+++ b/solution.py
@@ -11,6 +11,7 @@
 BLOCK = 128
 FAR = 1 << 30
 MIB = 1024 * 1024
+LOG2E = math.log2(math.e)
 SPARE = 8 * MIB
 
 scope = jax.named_scope
@@ -81,10 +82,10 @@
 def kernel(
     n, dn, scale,
     chosen, q_hbm, k_hbm, v_hbm, g_hbm, proj,
-    dq_r, dkv_r, w_out, mix_r,
+    dq_r, dkv_r, w_out, mix_r, kept_out,
     picked, qkv_in, g_in, qkv, g, kpos, qkv_r, g_r, proj_r, agp_s, agp_r, ag_s, ag_r,
     attn_s, attn_r, attn_y, attn_d, attn_e, attn_t,
-    p_s, k_t, v_t, dq_s, dkv_s, dk_acc, dv_acc, w_s, w_x, w_m, w_p, mix_s,
+    p_s, k_t, v_t, dq_s, dkv_s, dk_acc, dv_acc, w_c, w_s, w_x, w_m, w_p, mix_s,
     ss, rs, proj_rs, g_rs, agp_rs, ag_rs, ad_rs, ae_rs, loc,
 ):
     me = lax.axis_index("ctx")
@@ -144,6 +145,7 @@
     for t, src in enumerate((q_hbm, k_hbm, v_hbm)):
         pltpu.make_async_copy(src, qkv_in.at[t], loc.at[2]).start()
     own_proj.start()
+    pltpu.make_async_copy(chosen, kept_out, loc.at[11]).start()
     pick.wait()
     marks = block_marks(picked, me, qkv_in.shape[1] // block)
 
@@ -160,29 +162,31 @@
     def sent(view, send):
         ctx_copy(view, view, send, r_pp, pair).wait_send()
 
-    with scope("A_load"):
+    with scope("B_barrier"):
+        pl.semaphore_wait(barrier, n - 1 + dn - 1)
+
+    own_block = proj_r.at[side, row]
+    for a in [partner] + mates:
+        ctx_copy(proj, own_block, s_proj, proj_rs.at[row], 2 * a + side).start()
+
+    with scope("A_loadg"):
         g_load.wait()
         for j in range(dn):
             g[j] = chosen_rows(lambda r: g_in[r, j * dc:(j + 1) * dc])
         g_r[side, md] = g[md]
+    twin = md + 1 - 2 * lax.rem(md, 2)
+    dp_far = [lax.rem(md + 2 * s, dn) for s in range(1, dn // 2)]
+    dp_cross = [lax.rem(twin + 2 * s, dn) for s in range(1, dn // 2)]
+
+    for peer in dp_far + dp_cross + [twin]:
+        dp_copy(g.at[peer], g_r.at[side, md], s_g, g_rs.at[md], peer).start()
+    ctx_copy(g.at[md], g_r.at[side, md], s_gp, r_gp, pair).start()
+    with scope("A_loadqkv"):
         pltpu.make_async_copy(qkv_in, qkv_in, loc.at[2]).wait()
         for t in range(3):
             for h in range(n):
                 qkv[h, t] = chosen_rows(lambda r: qkv_in[t, r, h * dh:(h + 1) * dh])
         qkv_r[me] = qkv[me]
-    with scope("B_barrier"):
-        pl.semaphore_wait(barrier, n - 1 + dn - 1)
-
-    twin = md + 1 - 2 * lax.rem(md, 2)
-    dp_far = [lax.rem(md + 2 * s, dn) for s in range(1, dn // 2)]
-    dp_cross = [lax.rem(twin + 2 * s, dn) for s in range(1, dn // 2)]
-
-    own_block = proj_r.at[side, row]
-    for a in [partner] + mates:
-        ctx_copy(proj, own_block, s_proj, proj_rs.at[row], 2 * a + side).start()
-    for peer in dp_far + dp_cross + [twin]:
-        dp_copy(g.at[peer], g_r.at[side, md], s_g, g_rs.at[md], peer).start()
-    ctx_copy(g.at[md], g_r.at[side, md], s_gp, r_gp, pair).start()
 
     def send_qkv(peers):
         for peer in peers:
@@ -270,18 +274,16 @@
         i = ordered(k)
         q = qkv_r[pl.ds(2 * i, 2), 0].reshape(width, dh)
         keys = qkv_r[:, 1].reshape(slots, dh)
-        scores = dot_nt(keys, q) * scale
+        scores = dot_nt(keys, q)
         key_pos = kpos[...]
         key_pos = jnp.concatenate([key_pos, key_pos], axis=1)
-        same = lax.broadcasted_iota(jnp.int32, (slots, width), 0) == (
-            lax.broadcasted_iota(jnp.int32, (slots, width), 1) + i * width)
         lane = lax.broadcasted_iota(jnp.int32, (1, width), 1)
         one, two = picked[0, 2 * i], picked[0, 2 * i + 1]
         one = jnp.where(one >= 0, one * block, -FAR)
         two = jnp.where(two >= 0, (two - 1) * block, -FAR)
         query_pos = lane + jnp.where(lane < block, one, two)
-        scores = jnp.where((key_pos <= query_pos) | same, scores, -1e30)
-        e = jnp.exp(scores - jnp.max(scores, axis=0, keepdims=True))
+        scores = jnp.where(key_pos <= query_pos, scores * (scale * LOG2E), -1e30)
+        e = jnp.exp2(scores - jnp.max(scores, axis=0, keepdims=True))
         p = (e * (1.0 / jnp.sum(e, axis=0, keepdims=True))).astype(bf16)
         p_s[i] = p
         a_t = dot_nn(v_t[...], p)
@@ -377,19 +379,6 @@
     own_near = spread(attn_r.at[groups[1]], lambda d: attn_d.at[1, d, pl.ds(0, half)], s_ad, ad_rs.at[1], loc.at[7])
     ctx_copy(attn_r.at[:, pl.ds(pl.multiple_of(other * block, block), block)], attn_y, s_ap, r_ap, pair).start()
     send_dkv([2 * a + other for a in [partner] + mate_partners + mates] + [pair])
-    with scope("N_handover0"):
-        hand_over(lambda d: attn_d.at[0, d, pl.ds(0, half)], s_ad, ad_rs.at[0])
-    with scope("N_waitpair"):
-        arrived(attn_y, r_ap)
-    own_ae = spread(attn_y, lambda d: attn_e.at[d], s_ae, ae_rs, loc.at[8])
-    with scope("N_handover1"):
-        hand_over(lambda d: attn_d.at[1, d, pl.ds(0, half)], s_ad, ad_rs.at[1])
-    with scope("N_waitspread"):
-        own_far.wait()
-        own_near.wait()
-        for t in range(2):
-            arrived(attn_d.at[t, pl.ds(0, dn // 2)], ad_rs.at[t, 0])
-
     def weight(t, a):
         total = None
         for b in range(2):
@@ -402,26 +391,44 @@
         w_s[slot] = value.astype(bf16)
         ctx_copy(w_s.at[slot], dst, s_w, recv, 2 * peer_row + side).start()
 
+    def spread_done(t, own):
+        own.wait()
+        arrived(attn_d.at[t, pl.ds(0, dn // 2)], ad_rs.at[t, 0])
+
+    with scope("N_handover0"):
+        hand_over(lambda d: attn_d.at[0, d, pl.ds(0, half)], s_ad, ad_rs.at[0])
+    with scope("N_waitspread0"):
+        spread_done(0, own_far)
     with scope("P_weight"):
         for k, a in enumerate(mate_partners):
             send_w(k, weight(0, a), w_x.at[row], r_wx, mates[k])
-        crossing = weight(0, partner)
+    with scope("N_waitpair"):
+        arrived(attn_y, r_ap)
+    own_ae = spread(attn_y, lambda d: attn_e.at[d], s_ae, ae_rs, loc.at[8])
+    with scope("N_handover1"):
+        hand_over(lambda d: attn_d.at[1, d, pl.ds(0, half)], s_ad, ad_rs.at[1])
+    with scope("P_weight"):
+        w_c[...] = weight(0, partner)
+    with scope("N_waitspread1"):
+        spread_done(1, own_near)
+    with scope("P_weight"):
         for k, a in enumerate(mates):
             send_w(half - 1 + k, weight(1, a), w_m.at[row], r_wm, a)
         w_out[...] = weight(1, row)
-
-
-    def cross_sum(total):
+    inner = lax.rem(row, half) == (half - 1) * (1 - row // half)
+
+    def cross_sum():
         if mates:
             arrived(w_x.at[pl.ds(0, half - 1)], r_wx)
+        total = w_c[...]
         for a in mates:
             total = total + w_x[a].astype(jnp.float32)
         send_w(rows - 2, total, w_p, r_wp, partner)
 
+    with scope("S_waitinner"):
+        pl.when(inner)(cross_sum)
     with scope("O_handover"):
         hand_over(lambda d: attn_e.at[d], s_ae, ae_rs)
-    with scope("S_waitcross"):
-        cross_sum(crossing)
     with scope("O_waitrows"):
         arrived(proj_r.at[other], r_pp)
         own_ae.wait()
@@ -447,6 +454,9 @@
         dp_copy(mix_s.at[peer], mix_r.at[md], s_mix, r_mix, peer).start()
     own_mix = pltpu.make_async_copy(mix_s.at[md], mix_r.at[md], loc.at[9])
     own_mix.start()
+
+    with scope("S_waitcross"):
+        pl.when(jnp.logical_not(inner))(cross_sum)
 
     with scope("T_waitdq"):
         pltpu.make_async_copy(dq_s.at[me], dq_r.at[me], loc.at[4]).wait()
@@ -466,6 +476,7 @@
         own_mix.wait()
         arrived(mix_r.at[pl.ds(0, dn - 1)], r_mix)
 
+    pltpu.make_async_copy(chosen, kept_out, loc.at[11]).wait()
     with scope("Y_waitsend"):
         blocks = pl.ds(0, n - 1)
         others = pl.ds(0, dn - 1)
@@ -512,10 +523,10 @@
         ((dn, rows, BLOCK, dh), bf16), ((rows, dh, width), bf16),
         ((rows, slots, width), bf16), ((dh, slots), bf16), ((dh, slots), bf16),
         (blocks, bf16), ((n, 2, BLOCK, dh), bf16), ((slots, dh), f32), ((slots, dh), f32),
-        (sheets, bf16), (sheets, bf16), (sheets, bf16), ((dh, dc), bf16), ((dn, BLOCK, dc), bf16),
+        ((dh, dc), f32), (sheets, bf16), (sheets, bf16), (sheets, bf16), ((dh, dc), bf16), ((dn, BLOCK, dc), bf16),
     ]
     held = sum(math.prod(shape) * jnp.dtype(kind).itemsize for shape, kind in buffers)
-    sems = [sem((16,)), sem((12,)), sem((rows,)), sem((dn,)), sem((n,)), sem((rows,)), sem((2, dn // 2)), sem((dn // 2,)), sem((11,))]
+    sems = [sem((16,)), sem((12,)), sem((rows,)), sem((dn,)), sem((n,)), sem((rows,)), sem((2, dn // 2)), sem((dn // 2,)), sem((12,))]
     vmem = pl.BlockSpec(memory_space=pltpu.VMEM)
     picks = pltpu.SMEM(chosen.shape, chosen.dtype)
     free = pl.BlockSpec(memory_space=pl.ANY)
@@ -525,16 +536,17 @@
         return pltpu.with_memory_space_constraint(x, pltpu.HBM)
 
     chosen = kept(chosen)
-    dq, dkv, weight_grad, mixed = pl.pallas_call(
+    dq, dkv, weight_grad, mixed, placed = pl.pallas_call(
         functools.partial(kernel, n, dn, 1.0 / math.sqrt(dh)),
         out_shape=(
             jax.ShapeDtypeStruct(blocks, bf16),
             jax.ShapeDtypeStruct((n, 2, BLOCK, dh), bf16),
             jax.ShapeDtypeStruct((dh, dc), f32),
             jax.ShapeDtypeStruct((dn, BLOCK, dc), bf16),
+            jax.ShapeDtypeStruct(chosen.shape, chosen.dtype),
         ),
         in_specs=[hbm] * 6,
-        out_specs=[free, free, vmem, free],
+        out_specs=[free, free, vmem, free, free],
         scratch_shapes=[picks] + [pltpu.VMEM(shape, kind) for shape, kind in buffers] + sems,
         compiler_params=pltpu.CompilerParams(
             collective_id=0, has_side_effects=True, vmem_limit_bytes=min(held + SPARE, 60 * MIB)),
@@ -548,11 +560,11 @@
         out_shape=(
             jax.ShapeDtypeStruct(wide, bf16), jax.ShapeDtypeStruct(thin, bf16), jax.ShapeDtypeStruct(thin, bf16),
             jax.ShapeDtypeStruct(thin, bf16), jax.ShapeDtypeStruct((dh, dc), f32)),
-        in_specs=[hbm] + [free] * 4,
+        in_specs=[free] * 5,
         out_specs=[hbm] * 5,
         scratch_shapes=[picks, pltpu.VMEM((BLOCK, max(dn * dc, hd)), bf16), sem((count, 4)), sem((2,))],
         compiler_params=pltpu.CompilerParams(vmem_limit_bytes=8 * MIB),
-    )(chosen, mixed, dq, dkv, weight_grad)
+    )(placed, mixed, dq, dkv, weight_grad)
     return out[None], q_grad[None], k_grad[None], v_grad[None], proj_grad
 
 

time: 72.8 us -> 68.8 us (0.945)
  the two profiles are of different devices: /device:TPU:25 before, /device:TPU:13 now
where the time goes in v5:
time: 68.8 us; the launch traced here: 68.6 us
  Pallas kernels  68 us (99%)
    pallas_call x1, Pallas kernels, shards(): pl.pallas_call(functools.partial(kernel, n, dn, 1.0 / math.sqrt(dh)), out...  65.9 us
    pallas_call x1, Pallas kernels, shards(): pl.pallas_call(functools.partial(place_kernel, n, dn, count), out_shape=(...  2.12 us

profile of v5, /device:TPU:13, one launch (start us, length us, event | category | flops | bytes accessed | tf_op | source)
XLA Modules:
  0.0 68.6 jit_solution(17083007731797253828)
XLA Ops:
  0.6 65.9 %shard_map.101 = (bf16[8,128,128]{2,1,0:T(8,128)(2,1)S(1)}, bf16[8,2,128,128]{3,2,1,0:T(8,128)(2,1)S(1)}, f32[128,512]{1,0:T(8,128)S(1)}, bf16[4,128,512]{2,1,0:T(8,128)(2,1)S(1)}, s32[1,8]{1,0:T(1,128)S(1)}) custom-call(s32[1,8]{1,0:T(1,128)} %chosen.1, bf16[256,1024]{1,0:T(8,128)(2,1)} %bitcast.9, bf16[256,1024]{1,0:T(8,128)(2,1)} %bitcast.10, ...), custom_call_target="tpu_custom_call" | custom-call | tf_op jit(solution)/shard_map/pallas_call | solution.py:539
  66.5 2.1 %shard_map.102 = (bf16[256,2048]{1,0:T(8,128)(2,1)}, bf16[256,1024]{1,0:T(8,128)(2,1)}, bf16[256,1024]{1,0:T(8,128)(2,1)}, bf16[256,1024]{1,0:T(8,128)(2,1)}, f32[128,512]{1,0:T(8,128)}) custom-call(s32[1,8]{1,0:T(1,128)S(1)} %get-tuple-element.15.chosen, bf16[4,128,512]{2,1,0:T(8,128)(2,1)S(1)} %get-tuple-element.16.mix, ...), custom_call_target="tpu_custom_call" | custom-call | tf_op jit(solution)/shard_map/pallas_call | solution.py:558

commit v6 on v5

--- a/solution.py
+++ b/solution.py
@@ -29,54 +29,48 @@
     return a.astype(jnp.float32).T.astype(a.dtype)
 
 
-def local_block(picked, me, count):
-    entry = picked[0, me]
+def local_block(entry, me, count):
     spans = count // 2
     index = jnp.maximum(entry, 0)
-    local = jnp.where(index // spans == me, index % spans, spans + index % spans)
-    return entry, local
+    return jnp.where(index // spans == me, index % spans, spans + index % spans)
 
 
 def block_marks(picked, me, count):
-    entry, local = local_block(picked, me, count)
-    local = jnp.where(entry >= 0, local, -1)
+    entry = picked[0, me]
+    local = jnp.where(entry >= 0, local_block(entry, me, count), -1)
     return [jnp.where(local == j, 1.0, 0.0) for j in range(count)]
 
 
-def place_kernel(n, dn, count, chosen, mix, dq, dkv, w, out, q_out, k_out, v_out, w_out, picked, zero, sems, w_sem):
-    block, dh, dc = dq.shape[1], dq.shape[2], mix.shape[2]
-    pick = pltpu.make_async_copy(chosen, picked, w_sem.at[1])
-    pick.start()
+def place_kernel(count, chosen, mix, dq, dkv, w, out, q_out, k_out, v_out, w_out, zero, sems, w_sem):
+    block = dq.shape[0]
     w_copy = pltpu.make_async_copy(w, w_out, w_sem.at[0])
     w_copy.start()
     zero[...] = jnp.zeros_like(zero)
-    pick.wait()
-    entry, local = local_block(picked, lax.axis_index("ctx"), count)
-    local = jnp.where(entry >= 0, local, -1)
-    outs = (out, q_out, k_out, v_out)
-    for j in range(count):
-        rows = pl.ds(j * block, block)
-
-        @pl.when(local == j)
-        def _():
-            for d in range(dn):
-                pltpu.make_async_copy(mix.at[d], out.at[rows, pl.ds(d * dc, dc)], sems.at[j, 0]).start()
-            for h in range(n):
-                cols = pl.ds(h * dh, dh)
-                pltpu.make_async_copy(dq.at[h], q_out.at[rows, cols], sems.at[j, 1]).start()
-                pltpu.make_async_copy(dkv.at[h, 0], k_out.at[rows, cols], sems.at[j, 2]).start()
-                pltpu.make_async_copy(dkv.at[h, 1], v_out.at[rows, cols], sems.at[j, 3]).start()
-
-        @pl.when(local != j)
-        def _():
-            for t, dst in enumerate(outs):
-                pltpu.make_async_copy(zero.at[:, pl.ds(0, dst.shape[1])], dst.at[rows], sems.at[j, t]).start()
-
-    for j in range(count):
-        for t, dst in enumerate(outs):
-            view = dst.at[pl.ds(j * block, block)]
-            pltpu.make_async_copy(view, view, sems.at[j, t]).wait()
-    w_copy.wait()
+    me = lax.axis_index("ctx")
+    with scope("a_pick"):
+        lane = lax.broadcasted_iota(jnp.int32, chosen.shape, 1)
+        entry = jnp.max(jnp.where(lane == me, chosen[...], -1))
+        local = jnp.where(entry >= 0, local_block(entry, me, count), -1)
+    outs = ((mix, out), (dq, q_out), (dkv.at[0], k_out), (dkv.at[1], v_out))
+    with scope("b_issue"):
+        for j in range(count):
+            for t, (src, dst) in enumerate(outs):
+                rows = dst.at[pl.ds(j * block, block)]
+
+                @pl.when(local == j)
+                def _():
+                    pltpu.make_async_copy(src, rows, sems.at[j, t]).start()
+
+                @pl.when(local != j)
+                def _():
+                    pltpu.make_async_copy(zero.at[:, pl.ds(0, dst.shape[1])], rows, sems.at[j, t]).start()
+
+    with scope("c_wait"):
+        for j in range(count):
+            for t, (_, dst) in enumerate(outs):
+                view = dst.at[pl.ds(j * block, block)]
+                pltpu.make_async_copy(view, view, sems.at[j, t]).wait()
+        w_copy.wait()
 
 
 def kernel(
@@ -146,8 +140,6 @@
         pltpu.make_async_copy(src, qkv_in.at[t], loc.at[2]).start()
     own_proj.start()
     pltpu.make_async_copy(chosen, kept_out, loc.at[11]).start()
-    pick.wait()
-    marks = block_marks(picked, me, qkv_in.shape[1] // block)
 
     def chosen_rows(load):
         total = None
@@ -170,6 +162,8 @@
         ctx_copy(proj, own_block, s_proj, proj_rs.at[row], 2 * a + side).start()
 
     with scope("A_loadg"):
+        pick.wait()
+        marks = block_marks(picked, me, qkv_in.shape[1] // block)
         g_load.wait()
         for j in range(dn):
             g[j] = chosen_rows(lambda r: g_in[r, j * dc:(j + 1) * dc])
@@ -249,13 +243,14 @@
         for a in mates:
             proj_arrived(a)
     parts([partner] + mates + [row], side, waiting, n)
+    with scope("F_waitpairg"):
+        arrived(g_r.at[other], r_gp)
+    parts([partner] + mates + [row], other, waiting, n)
     with scope("F_waitsecond"):
         for a in mate_partners:
             proj_arrived(a)
-    parts(mate_partners, side, waiting, n)
-    with scope("F_waitpairg"):
-        arrived(g_r.at[other], r_gp)
-    parts([partner] + mate_partners + mates + [row], other, waiting, rows)
+    for b in (side, other):
+        parts(mate_partners, b, waiting, rows)
     with scope("H_finish"):
         for a, b in waiting:
             finish(a, b)
@@ -310,6 +305,9 @@
     dk_acc[...] = jnp.zeros_like(dk_acc)
     dv_acc[...] = jnp.zeros_like(dv_acc)
 
+    def heads_of_me(ref):
+        return ref.at[:, pl.ds(pl.multiple_of(me * dh, dh), dh)]
+
     def backward(k, carry):
         i = ordered(k)
         with scope("K_waitag"):
@@ -330,11 +328,11 @@
 
             @pl.when(peer != me)
             def _():
-                ctx_copy(dq_s.at[peer], dq_r.at[me], s_dq, r_dq, peer).start()
+                ctx_copy(dq_s.at[peer], heads_of_me(dq_r), s_dq, r_dq, peer).start()
 
             @pl.when(peer == me)
             def _():
-                pltpu.make_async_copy(dq_s.at[peer], dq_r.at[peer], loc.at[4]).start()
+                pltpu.make_async_copy(dq_s.at[peer], heads_of_me(dq_r), loc.at[4]).start()
 
         dk_acc[...] += dot_nn(ds, q)
         dv_acc[...] += dot_nn(p, da)
@@ -346,12 +344,14 @@
     dkv_s[:, 0] = (dk_acc[...] * scale).astype(bf16).reshape(n, block, dh)
     dkv_s[:, 1] = dv_acc[...].astype(bf16).reshape(n, block, dh)
 
+    my_dkv = dkv_r.at[:, :, pl.ds(pl.multiple_of(me * dh, dh), dh)]
+
     def send_dkv(peers):
         for peer in peers:
-            ctx_copy(dkv_s.at[peer], dkv_r.at[me], s_dkv, r_dkv, peer).start()
+            ctx_copy(dkv_s.at[peer], my_dkv, s_dkv, r_dkv, peer).start()
 
     send_dkv([2 * a + side for a in [partner] + mate_partners + mates])
-    own_dkv = pltpu.make_async_copy(dkv_s.at[me], dkv_r.at[me], loc.at[5])
+    own_dkv = pltpu.make_async_copy(dkv_s.at[me], my_dkv, loc.at[5])
     own_dkv.start()
 
     def spread(src, dst_of, send, recv, own_sem):
@@ -448,22 +448,23 @@
         mix_s[d] = out.astype(bf16).reshape(2, block, dc)
         return carry
 
+    my_columns = mix_r.at[:, pl.ds(pl.multiple_of(md * dc, dc), dc)]
     with scope("Q_mix"):
         lax.fori_loop(0, dn // 2, mix_step, 0)
     for peer in dp_peers:
-        dp_copy(mix_s.at[peer], mix_r.at[md], s_mix, r_mix, peer).start()
-    own_mix = pltpu.make_async_copy(mix_s.at[md], mix_r.at[md], loc.at[9])
+        dp_copy(mix_s.at[peer], my_columns, s_mix, r_mix, peer).start()
+    own_mix = pltpu.make_async_copy(mix_s.at[md], my_columns, loc.at[9])
     own_mix.start()
 
     with scope("S_waitcross"):
         pl.when(jnp.logical_not(inner))(cross_sum)
 
     with scope("T_waitdq"):
-        pltpu.make_async_copy(dq_s.at[me], dq_r.at[me], loc.at[4]).wait()
-        arrived(dq_r.at[pl.ds(0, n - 1)], r_dq)
+        pltpu.make_async_copy(dq_s.at[me], heads_of_me(dq_r), loc.at[4]).wait()
+        arrived(dq_r.at[:, pl.ds(0, (n - 1) * dh)], r_dq)
     with scope("U_waitdkv"):
         own_dkv.wait()
-        arrived(dkv_r.at[pl.ds(0, n - 1)], r_dkv)
+        arrived(dkv_r.at[:, :, pl.ds(0, (n - 1) * dh)], r_dkv)
     with scope("W_waitmates"):
         if mates:
             arrived(w_m.at[pl.ds(0, half - 1)], r_wm)
@@ -474,7 +475,7 @@
         w_out[...] += w_p[...].astype(jnp.float32)
     with scope("V_waitmix"):
         own_mix.wait()
-        arrived(mix_r.at[pl.ds(0, dn - 1)], r_mix)
+        arrived(mix_r.at[:, pl.ds(0, (dn - 1) * dc)], r_mix)
 
     pltpu.make_async_copy(chosen, kept_out, loc.at[11]).wait()
     with scope("Y_waitsend"):
@@ -539,10 +540,10 @@
     dq, dkv, weight_grad, mixed, placed = pl.pallas_call(
         functools.partial(kernel, n, dn, 1.0 / math.sqrt(dh)),
         out_shape=(
-            jax.ShapeDtypeStruct(blocks, bf16),
-            jax.ShapeDtypeStruct((n, 2, BLOCK, dh), bf16),
+            jax.ShapeDtypeStruct((BLOCK, hd), bf16),
+            jax.ShapeDtypeStruct((2, BLOCK, hd), bf16),
             jax.ShapeDtypeStruct((dh, dc), f32),
-            jax.ShapeDtypeStruct((dn, BLOCK, dc), bf16),
+            jax.ShapeDtypeStruct((BLOCK, dn * dc), bf16),
             jax.ShapeDtypeStruct(chosen.shape, chosen.dtype),
         ),
         in_specs=[hbm] * 6,
@@ -556,13 +557,13 @@
     thin = (tokens, hd)
     count = tokens // BLOCK
     out, q_grad, k_grad, v_grad, proj_grad = pl.pallas_call(
-        functools.partial(place_kernel, n, dn, count),
+        functools.partial(place_kernel, count),
         out_shape=(
             jax.ShapeDtypeStruct(wide, bf16), jax.ShapeDtypeStruct(thin, bf16), jax.ShapeDtypeStruct(thin, bf16),
             jax.ShapeDtypeStruct(thin, bf16), jax.ShapeDtypeStruct((dh, dc), f32)),
-        in_specs=[free] * 5,
+        in_specs=[vmem] + [free] * 4,
         out_specs=[hbm] * 5,
-        scratch_shapes=[picks, pltpu.VMEM((BLOCK, max(dn * dc, hd)), bf16), sem((count, 4)), sem((2,))],
+        scratch_shapes=[pltpu.VMEM((BLOCK, max(dn * dc, hd)), bf16), sem((count, 4)), sem((1,))],
         compiler_params=pltpu.CompilerParams(vmem_limit_bytes=8 * MIB),
     )(placed, mixed, dq, dkv, weight_grad)
     return out[None], q_grad[None], k_grad[None], v_grad[None], proj_grad

time: 68.8 us -> 68.8 us (level)
  the two profiles are of different devices: /device:TPU:13 before, /device:TPU:0 now
where the time goes in v6:
time: 68.8 us; the launch traced here: 68.1 us
  Pallas kernels  67.5 us (98%)
    pallas_call x1, Pallas kernels, shards(): pl.pallas_call(functools.partial(kernel, n, dn, 1.0 / math.sqrt(dh)), out...  65.7 us
    pallas_call x1, Pallas kernels, shards(): pl.pallas_call(functools.partial(place_kernel, count), out_shape=(jax.Sha...  1.77 us

profile of v6, /device:TPU:0, one launch (start us, length us, event | category | flops | bytes accessed | tf_op | source)
XLA Modules:
  0.0 68.1 jit_solution(16569520021140121178)
XLA Ops:
  0.6 65.7 %shard_map.101 = (bf16[128,1024]{1,0:T(8,128)(2,1)S(1)}, bf16[2,128,1024]{2,1,0:T(8,128)(2,1)S(1)}, f32[128,512]{1,0:T(8,128)S(1)}, bf16[128,2048]{1,0:T(8,128)(2,1)S(1)}, s32[1,8]{1,0:T(1,128)S(1)}) custom-call(s32[1,8]{1,0:T(1,128)} %chosen.1, bf16[256,1024]{1,0:T(8,128)(2,1)} %bitcast.9, bf16[256,1024]{1,0:T(8,128)(2,1)} %bitcast.10, ...), custom_call_target="tpu_custom_call" | custom-call | tf_op jit(solution)/shard_map/pallas_call | solution.py:540
  66.3 1.8 %shard_map.102 = (bf16[256,2048]{1,0:T(8,128)(2,1)}, bf16[256,1024]{1,0:T(8,128)(2,1)}, bf16[256,1024]{1,0:T(8,128)(2,1)}, bf16[256,1024]{1,0:T(8,128)(2,1)}, f32[128,512]{1,0:T(8,128)}) custom-call(s32[1,8]{1,0:T(1,128)S(1)} %get-tuple-element.15.chosen, bf16[128,2048]{1,0:T(8,128)(2,1)S(1)} %get-tuple-element.16.mix, ...), custom_call_target="tpu_custom_call" | custom-call | tf_op jit(solution)/shard_map/pallas_call | solution.py:559

commit v7 on v6

--- a/solution.py
+++ b/solution.py
@@ -350,7 +350,8 @@
         for peer in peers:
             ctx_copy(dkv_s.at[peer], my_dkv, s_dkv, r_dkv, peer).start()
 
-    send_dkv([2 * a + side for a in [partner] + mate_partners + mates])
+    far_rows = [k + (rows - 1 - 2 * k) * (1 - row // half) for k in range(half)]
+    send_dkv([2 * a + side for a in far_rows + mates])
     own_dkv = pltpu.make_async_copy(dkv_s.at[me], my_dkv, loc.at[5])
     own_dkv.start()
 
@@ -378,7 +379,10 @@
         pltpu.make_async_copy(attn_s.at[row], attn_r.at[row], loc.at[3]).wait()
     own_near = spread(attn_r.at[groups[1]], lambda d: attn_d.at[1, d, pl.ds(0, half)], s_ad, ad_rs.at[1], loc.at[7])
     ctx_copy(attn_r.at[:, pl.ds(pl.multiple_of(other * block, block), block)], attn_y, s_ap, r_ap, pair).start()
-    send_dkv([2 * a + other for a in [partner] + mate_partners + mates] + [pair])
+
+    inner = lax.rem(row, half) == (half - 1) * (1 - row // half)
+
+    send_dkv([2 * a + other for a in far_rows + mates] + [pair])
     def weight(t, a):
         total = None
         for b in range(2):
@@ -397,38 +401,40 @@
 
     with scope("N_handover0"):
         hand_over(lambda d: attn_d.at[0, d, pl.ds(0, half)], s_ad, ad_rs.at[0])
-    with scope("N_waitspread0"):
-        spread_done(0, own_far)
-    with scope("P_weight"):
-        for k, a in enumerate(mate_partners):
-            send_w(k, weight(0, a), w_x.at[row], r_wx, mates[k])
     with scope("N_waitpair"):
         arrived(attn_y, r_ap)
     own_ae = spread(attn_y, lambda d: attn_e.at[d], s_ae, ae_rs, loc.at[8])
     with scope("N_handover1"):
         hand_over(lambda d: attn_d.at[1, d, pl.ds(0, half)], s_ad, ad_rs.at[1])
+    with scope("N_waitspread0"):
+        spread_done(0, own_far)
     with scope("P_weight"):
-        w_c[...] = weight(0, partner)
+        for k, a in enumerate(far_rows):
+            w_c[k] = weight(0, a)
+
+        @pl.when(jnp.logical_not(inner))
+        def _():
+            for k in range(half):
+                send_w(k, w_c[k], w_x.at[lax.rem(row, half), k], r_wx, own_base + (half - 1) * (1 - row // half))
     with scope("N_waitspread1"):
         spread_done(1, own_near)
     with scope("P_weight"):
         for k, a in enumerate(mates):
-            send_w(half - 1 + k, weight(1, a), w_m.at[row], r_wm, a)
+            send_w(half + k, weight(1, a), w_m.at[row], r_wm, a)
         w_out[...] = weight(1, row)
-    inner = lax.rem(row, half) == (half - 1) * (1 - row // half)
-
     def cross_sum():
         if mates:
             arrived(w_x.at[pl.ds(0, half - 1)], r_wx)
-        total = w_c[...]
-        for a in mates:
-            total = total + w_x[a].astype(jnp.float32)
-        send_w(rows - 2, total, w_p, r_wp, partner)
-
+        for k, a in enumerate(far_rows):
+            total = w_c[k]
+            for mate in mates:
+                total = total + w_x[lax.rem(mate, half), k].astype(jnp.float32)
+            send_w(k, total, w_p, r_wp, a)
+
+    with scope("O_handover"):
+        hand_over(lambda d: attn_e.at[d], s_ae, ae_rs)
     with scope("S_waitinner"):
         pl.when(inner)(cross_sum)
-    with scope("O_handover"):
-        hand_over(lambda d: attn_e.at[d], s_ae, ae_rs)
     with scope("O_waitrows"):
         arrived(proj_r.at[other], r_pp)
         own_ae.wait()
@@ -436,7 +442,9 @@
 
     mine = pl.ds(pl.multiple_of(side * block, block), block)
 
-    def mix_step(j, carry):
+    def mix_step(k, carry):
+        j = lax.rem(md // 2 + 1 + k, dn // 2)
+
         def two(ref, *at):
             return ref[at].reshape(width, dh)
 
@@ -446,18 +454,22 @@
         there = jnp.concatenate([two(attn_e, d, a) for a in range(rows)], axis=1)
         out = dot_nn(here, proj_r[side].reshape(rows * dh, dc)) + dot_nn(there, proj_r[other].reshape(rows * dh, dc))
         mix_s[d] = out.astype(bf16).reshape(2, block, dc)
+        for t in range(2):
+            peer = 2 * j + t
+
+            @pl.when(peer != md)
+            def _():
+                dp_copy(mix_s.at[peer], my_columns, s_mix, r_mix, peer).start()
+
+            @pl.when(peer == md)
+            def _():
+                pltpu.make_async_copy(mix_s.at[peer], my_columns, loc.at[9]).start()
+
         return carry
 
     my_columns = mix_r.at[:, pl.ds(pl.multiple_of(md * dc, dc), dc)]
     with scope("Q_mix"):
         lax.fori_loop(0, dn // 2, mix_step, 0)
-    for peer in dp_peers:
-        dp_copy(mix_s.at[peer], my_columns, s_mix, r_mix, peer).start()
-    own_mix = pltpu.make_async_copy(mix_s.at[md], my_columns, loc.at[9])
-    own_mix.start()
-
-    with scope("S_waitcross"):
-        pl.when(jnp.logical_not(inner))(cross_sum)
 
     with scope("T_waitdq"):
         pltpu.make_async_copy(dq_s.at[me], heads_of_me(dq_r), loc.at[4]).wait()
@@ -474,7 +486,7 @@
         arrived(w_p, r_wp)
         w_out[...] += w_p[...].astype(jnp.float32)
     with scope("V_waitmix"):
-        own_mix.wait()
+        pltpu.make_async_copy(mix_s.at[md], my_columns, loc.at[9]).wait()
         arrived(mix_r.at[:, pl.ds(0, (dn - 1) * dc)], r_mix)
 
     pltpu.make_async_copy(chosen, kept_out, loc.at[11]).wait()
@@ -524,7 +536,7 @@
         ((dn, rows, BLOCK, dh), bf16), ((rows, dh, width), bf16),
         ((rows, slots, width), bf16), ((dh, slots), bf16), ((dh, slots), bf16),
         (blocks, bf16), ((n, 2, BLOCK, dh), bf16), ((slots, dh), f32), ((slots, dh), f32),
-        ((dh, dc), f32), (sheets, bf16), (sheets, bf16), (sheets, bf16), ((dh, dc), bf16), ((dn, BLOCK, dc), bf16),
+        ((half, dh, dc), f32), (sheets, bf16), ((half, half, dh, dc), bf16), (sheets, bf16), ((dh, dc), bf16), ((dn, BLOCK, dc), bf16),
     ]
     held = sum(math.prod(shape) * jnp.dtype(kind).itemsize for shape, kind in buffers)
     sems = [sem((16,)), sem((12,)), sem((rows,)), sem((dn,)), sem((n,)), sem((rows,)), sem((2, dn // 2)), sem((dn // 2,)), sem((12,))]

time: 68.8 us -> 68 us (0.988)
  Pallas kernels: 67.5 us -> 66.7 us
    pallas_call x1, Pallas kernels: 65.7 us -> 65 us  [shards(): pl.pallas_call(functools.partial(kernel, n, dn, 1.0 / math.sqrt(dh)), out...]
where the time goes in v7:
time: 68 us; the launch traced here: 67.4 us
  Pallas kernels  66.7 us (98%)
    pallas_call x1, Pallas kernels, shards(): pl.pallas_call(functools.partial(kernel, n, dn, 1.0 / math.sqrt(dh)), out...  65 us
    pallas_call x1, Pallas kernels, shards(): pl.pallas_call(functools.partial(place_kernel, count), out_shape=(jax.Sha...  1.77 us

profile of v7, /device:TPU:0, one launch (start us, length us, event | category | flops | bytes accessed | tf_op | source)
XLA Modules:
  0.0 67.4 jit_solution(5854478144575513615)
XLA Ops:
  0.6 65.0 %shard_map.101 = (bf16[128,1024]{1,0:T(8,128)(2,1)S(1)}, bf16[2,128,1024]{2,1,0:T(8,128)(2,1)S(1)}, f32[128,512]{1,0:T(8,128)S(1)}, bf16[128,2048]{1,0:T(8,128)(2,1)S(1)}, s32[1,8]{1,0:T(1,128)S(1)}) custom-call(s32[1,8]{1,0:T(1,128)} %chosen.1, bf16[256,1024]{1,0:T(8,128)(2,1)} %bitcast.9, bf16[256,1024]{1,0:T(8,128)(2,1)} %bitcast.10, ...), custom_call_target="tpu_custom_call" | custom-call | tf_op jit(solution)/shard_map/pallas_call | solution.py:552
  65.6 1.8 %shard_map.102 = (bf16[256,2048]{1,0:T(8,128)(2,1)}, bf16[256,1024]{1,0:T(8,128)(2,1)}, bf16[256,1024]{1,0:T(8,128)(2,1)}, bf16[256,1024]{1,0:T(8,128)(2,1)}, f32[128,512]{1,0:T(8,128)}) custom-call(s32[1,8]{1,0:T(1,128)S(1)} %get-tuple-element.15.chosen, bf16[128,2048]{1,0:T(8,128)(2,1)S(1)} %get-tuple-element.16.mix, ...), custom_call_target="tpu_custom_call" | custom-call | tf_op jit(solution)/shard_map/pallas_call | solution.py:571

commit v8 on v7

--- a/solution.py
+++ b/solution.py
@@ -351,7 +351,6 @@
             ctx_copy(dkv_s.at[peer], my_dkv, s_dkv, r_dkv, peer).start()
 
     far_rows = [k + (rows - 1 - 2 * k) * (1 - row // half) for k in range(half)]
-    send_dkv([2 * a + side for a in far_rows + mates])
     own_dkv = pltpu.make_async_copy(dkv_s.at[me], my_dkv, loc.at[5])
     own_dkv.start()
 
@@ -382,7 +381,7 @@
 
     inner = lax.rem(row, half) == (half - 1) * (1 - row // half)
 
-    send_dkv([2 * a + other for a in far_rows + mates] + [pair])
+    send_dkv([2 * a + s for s in (side, other) for a in far_rows + mates] + [pair])
     def weight(t, a):
         total = None
         for b in range(2):

time: 68 us -> 67.8 us (level)
  no operation moved by 1% of the time
where the time goes in v8:
time: 67.8 us; the launch traced here: 67.6 us
  Pallas kernels  67 us (99%)
    pallas_call x1, Pallas kernels, shards(): pl.pallas_call(functools.partial(kernel, n, dn, 1.0 / math.sqrt(dh)), out...  65.2 us
    pallas_call x1, Pallas kernels, shards(): pl.pallas_call(functools.partial(place_kernel, count), out_shape=(jax.Sha...  1.77 us

profile of v8, /device:TPU:0, one launch (start us, length us, event | category | flops | bytes accessed | tf_op | source)
XLA Modules:
  0.0 67.6 jit_solution(3523423900889753212)
XLA Ops:
  0.6 65.2 %shard_map.101 = (bf16[128,1024]{1,0:T(8,128)(2,1)S(1)}, bf16[2,128,1024]{2,1,0:T(8,128)(2,1)S(1)}, f32[128,512]{1,0:T(8,128)S(1)}, bf16[128,2048]{1,0:T(8,128)(2,1)S(1)}, s32[1,8]{1,0:T(1,128)S(1)}) custom-call(s32[1,8]{1,0:T(1,128)} %chosen.1, bf16[256,1024]{1,0:T(8,128)(2,1)} %bitcast.9, bf16[256,1024]{1,0:T(8,128)(2,1)} %bitcast.10, ...), custom_call_target="tpu_custom_call" | custom-call | tf_op jit(solution)/shard_map/pallas_call | solution.py:551
  65.8 1.8 %shard_map.102 = (bf16[256,2048]{1,0:T(8,128)(2,1)}, bf16[256,1024]{1,0:T(8,128)(2,1)}, bf16[256,1024]{1,0:T(8,128)(2,1)}, bf16[256,1024]{1,0:T(8,128)(2,1)}, f32[128,512]{1,0:T(8,128)}) custom-call(s32[1,8]{1,0:T(1,128)S(1)} %get-tuple-element.15.chosen, bf16[128,2048]{1,0:T(8,128)(2,1)S(1)} %get-tuple-element.16.mix, ...), custom_call_target="tpu_custom_call" | custom-call | tf_op jit(solution)/shard_map/pallas_call | solution.py:570

commit v9 on v8

--- a/solution.py
+++ b/solution.py
@@ -79,7 +79,7 @@
     dq_r, dkv_r, w_out, mix_r, kept_out,
     picked, qkv_in, g_in, qkv, g, kpos, qkv_r, g_r, proj_r, agp_s, agp_r, ag_s, ag_r,
     attn_s, attn_r, attn_y, attn_d, attn_e, attn_t,
-    p_s, k_t, v_t, dq_s, dkv_s, dk_acc, dv_acc, w_c, w_s, w_x, w_m, w_p, mix_s,
+    p_s, k_t, v_t, dq_s, dkv_s, dk_acc, dv_acc, w_c, w_s, w_x, w_m, w_p, mix_s, mix_acc,
     ss, rs, proj_rs, g_rs, agp_rs, ag_rs, ad_rs, ae_rs, loc,
 ):
     me = lax.axis_index("ctx")
@@ -434,24 +434,31 @@
         hand_over(lambda d: attn_e.at[d], s_ae, ae_rs)
     with scope("S_waitinner"):
         pl.when(inner)(cross_sum)
+    mine = pl.ds(pl.multiple_of(side * block, block), block)
+
+    def two(ref, *at):
+        return ref[at].reshape(width, dh)
+
+    def mix_here(j, carry):
+        d = pl.ds(2 * j, 2)
+        t_of = [row // half if a // half else 1 - row // half for a in range(rows)]
+        here = jnp.concatenate([two(attn_d, t_of[a], d, a % half, mine) for a in range(rows)], axis=1)
+        mix_acc[j] = dot_nn(here, proj_r[side].reshape(rows * dh, dc))
+        return carry
+
+    with scope("Q_here"):
+        lax.fori_loop(0, dn // 2, mix_here, 0)
     with scope("O_waitrows"):
         arrived(proj_r.at[other], r_pp)
         own_ae.wait()
         arrived(attn_e.at[pl.ds(0, dn // 2)], ae_rs.at[0])
 
-    mine = pl.ds(pl.multiple_of(side * block, block), block)
-
     def mix_step(k, carry):
         j = lax.rem(md // 2 + 1 + k, dn // 2)
 
-        def two(ref, *at):
-            return ref[at].reshape(width, dh)
-
         d = pl.ds(2 * j, 2)
-        t_of = [row // half if a // half else 1 - row // half for a in range(rows)]
-        here = jnp.concatenate([two(attn_d, t_of[a], d, a % half, mine) for a in range(rows)], axis=1)
         there = jnp.concatenate([two(attn_e, d, a) for a in range(rows)], axis=1)
-        out = dot_nn(here, proj_r[side].reshape(rows * dh, dc)) + dot_nn(there, proj_r[other].reshape(rows * dh, dc))
+        out = mix_acc[j] + dot_nn(there, proj_r[other].reshape(rows * dh, dc))
         mix_s[d] = out.astype(bf16).reshape(2, block, dc)
         for t in range(2):
             peer = 2 * j + t
@@ -536,6 +543,7 @@
         ((rows, slots, width), bf16), ((dh, slots), bf16), ((dh, slots), bf16),
         (blocks, bf16), ((n, 2, BLOCK, dh), bf16), ((slots, dh), f32), ((slots, dh), f32),
         ((half, dh, dc), f32), (sheets, bf16), ((half, half, dh, dc), bf16), (sheets, bf16), ((dh, dc), bf16), ((dn, BLOCK, dc), bf16),
+        ((dn // 2, width, dc), f32),
     ]
     held = sum(math.prod(shape) * jnp.dtype(kind).itemsize for shape, kind in buffers)
     sems = [sem((16,)), sem((12,)), sem((rows,)), sem((dn,)), sem((n,)), sem((rows,)), sem((2, dn // 2)), sem((dn // 2,)), sem((12,))]

time: 67.8 us -> 67.8 us (level)
  no operation moved by 1% of the time
where the time goes in v9:
time: 67.8 us; the launch traced here: 67.6 us
  Pallas kernels  67 us (99%)
    pallas_call x1, Pallas kernels, shards(): pl.pallas_call(functools.partial(kernel, n, dn, 1.0 / math.sqrt(dh)), out...  65.2 us
    pallas_call x1, Pallas kernels, shards(): pl.pallas_call(functools.partial(place_kernel, count), out_shape=(jax.Sha...  1.77 us

profile of v9, /device:TPU:0, one launch (start us, length us, event | category | flops | bytes accessed | tf_op | source)
XLA Modules:
  0.0 67.6 jit_solution(10928169220307240816)
XLA Ops:
  0.6 65.2 %shard_map.101 = (bf16[128,1024]{1,0:T(8,128)(2,1)S(1)}, bf16[2,128,1024]{2,1,0:T(8,128)(2,1)S(1)}, f32[128,512]{1,0:T(8,128)S(1)}, bf16[128,2048]{1,0:T(8,128)(2,1)S(1)}, s32[1,8]{1,0:T(1,128)S(1)}) custom-call(s32[1,8]{1,0:T(1,128)} %chosen.1, bf16[256,1024]{1,0:T(8,128)(2,1)} %bitcast.9, bf16[256,1024]{1,0:T(8,128)(2,1)} %bitcast.10, ...), custom_call_target="tpu_custom_call" | custom-call | tf_op jit(solution)/shard_map/pallas_call | solution.py:559
  65.8 1.8 %shard_map.102 = (bf16[256,2048]{1,0:T(8,128)(2,1)}, bf16[256,1024]{1,0:T(8,128)(2,1)}, bf16[256,1024]{1,0:T(8,128)(2,1)}, bf16[256,1024]{1,0:T(8,128)(2,1)}, f32[128,512]{1,0:T(8,128)}) custom-call(s32[1,8]{1,0:T(1,128)S(1)} %get-tuple-element.15.chosen, bf16[128,2048]{1,0:T(8,128)(2,1)S(1)} %get-tuple-element.16.mix, ...), custom_call_target="tpu_custom_call" | custom-call | tf_op jit(solution)/shard_map/pallas_call | solution.py:578
